TPU v7x, 32 devices: a whole 2x2x4 slice. The times are simulated.
32 devices in a mesh: dp: 8 (over z, y), tensor: 4 (over x, core).
Axes of the slice: x: 2, y: 2, z: 4, core: 2. Of those that a mesh axis runs over, the one named last changes fastest.
Arguments:
- tokens: int32 [16384], P('dp'), may hold values from 0 to 8190
- lengths: int32 [16, 4], P('dp'), may hold values from 1 to 512, 1024 in all within a row
- timesteps: int32 [16], P('dp'), may hold values from 1 to 1000, as said below
- masks: int32 [16384], P('dp'), may hold values from 0 to 1, as said below
- step_count: int32 [1], replicated, may hold values from 2 to 20
- table: float32 [8192, 768], P('tensor', 'dp'), may hold values from -0.4375 to 0.4375
- joint_weight: float32 [768, 2304], P('dp', 'tensor'), may hold values from -0.21875 to 0.21875
- output_weight: float32 [768, 768], P('tensor', 'dp'), may hold values from -1.75 to 1.75
- upward_weight: float32 [768, 3072], P('dp', 'tensor'), may hold values from -0.21875 to 0.21875
- downward_weight: float32 [3072, 768], P('tensor', 'dp'), may hold values from -0.21875 to 0.21875
- gains: float32 [3, 768], P(None, 'dp'), may hold values from 0.5 to 1.5
- momentum_table: float32 [8192, 768], P('tensor', 'dp'), may hold values from -3.8146973e-06 to 3.8146973e-06
- momentum_joint: float32 [768, 2304], P('dp', 'tensor'), may hold values from -3.8146973e-06 to 3.8146973e-06
- momentum_output: float32 [768, 768], P('tensor', 'dp'), may hold values from -3.8146973e-06 to 3.8146973e-06
- momentum_upward: float32 [768, 3072], P('dp', 'tensor'), may hold values from -3.8146973e-06 to 3.8146973e-06
- momentum_downward: float32 [3072, 768], P('tensor', 'dp'), may hold values from -3.8146973e-06 to 3.8146973e-06
- momentum_gains: float32 [3, 768], P(None, 'dp'), may hold values from -1.9073486e-05 to 1.9073486e-05
- variance_table: float32 [8192, 768], P('tensor', 'dp'), may hold values from 2.9919196e-14 to 1.1967678e-13
- variance_joint: float32 [768, 2304], P('dp', 'tensor'), may hold values from 2.9919196e-14 to 1.1967678e-13
- variance_output: float32 [768, 768], P('tensor', 'dp'), may hold values from 2.9919196e-14 to 1.1967678e-13
- variance_upward: float32 [768, 3072], P('dp', 'tensor'), may hold values from 2.9919196e-14 to 1.1967678e-13
- variance_downward: float32 [3072, 768], P('tensor', 'dp'), may hold values from 2.9919196e-14 to 1.1967678e-13
- variance_gains: float32 [3, 768], P(None, 'dp'), may hold values from 7.4797986e-13 to 2.9919194e-12
Outputs:
- loss: float32 [], replicated
- grad_norm: float32 [], replicated
- new_momentum_table: float32 [8192, 768], P('tensor', 'dp')
- new_variance_table: float32 [8192, 768], P('tensor', 'dp')
- new_table: float32 [8192, 768], P('tensor', 'dp')
- new_momentum_joint: float32 [768, 2304], P('dp', 'tensor')
- new_variance_joint: float32 [768, 2304], P('dp', 'tensor')
- new_joint: float32 [768, 2304], P('dp', 'tensor')
- new_momentum_output: float32 [768, 768], P('tensor', 'dp')
- new_variance_output: float32 [768, 768], P('tensor', 'dp')
- new_output: float32 [768, 768], P('tensor', 'dp')
- new_momentum_upward: float32 [768, 3072], P('dp', 'tensor')
- new_variance_upward: float32 [768, 3072], P('dp', 'tensor')
- new_upward: float32 [768, 3072], P('dp', 'tensor')
- new_momentum_downward: float32 [3072, 768], P('tensor', 'dp')
- new_variance_downward: float32 [3072, 768], P('tensor', 'dp')
- new_downward: float32 [3072, 768], P('tensor', 'dp')
- new_momentum_gains: float32 [3, 768], P(None, 'dp')
- new_variance_gains: float32 [3, 768], P(None, 'dp')
- new_gains: float32 [3, 768], P(None, 'dp')
Inputs may be any that keep to these rules, and one draw needn't show every extreme that they name: `timesteps`: a sequence's timestep is drawn uniformly; some sequence has timestep 1 and some has 1000. `masks`: each position of sequence s is masked independently with probability timesteps[s] / 1000.
All inputs are finite; a program needn't handle non-finite values.
Results may differ from a plain program's by a relative error of at most 0.0082.
Values may be sent and summed in bfloat16 or wider, within the bound.
A program may use at most 192 MiB of HBM per device.

v0:
```python
import jax
import jax.numpy as jnp
from jax import lax
from jax.sharding import PartitionSpec as P

D = 768
HEAD_DIM = 64
VOCAB = 8192
SEQ_LEN = 1024
DOCS = 4
T_DIFF = 1000


eps_norm = 1e-06
neg_fill = -1000000000.0
beta_one = 0.9
beta_two = 0.999
adam_eps = 1e-08
clip_at = 0.02
rates = (0.05, 0.03, 0.25, 0.03, 0.03, 0.3)
decays = (0.1, 0.1, 0.1, 0.1, 0.1, 0.0)


def joined(value, axis, join):
    pieces = jax.tree.map(lambda part: lax.all_gather(part, axis), value)
    head = jax.tree.map(lambda part: part[0], pieces)
    tail = jax.tree.map(lambda part: part[1:], pieces)
    running, _ = lax.scan(lambda running, piece: (join(running, piece), None), head, tail)
    return running


def tensor_total(partial_value):
    return lax.psum(partial_value, "tensor")


def norm_apply(values, gain):
    inverse = lax.rsqrt(jnp.mean(values * values, axis=-1, keepdims=True) + eps_norm)
    return values * inverse * gain


def norm_back(values, gain, upstream):
    inverse = lax.rsqrt(jnp.mean(values * values, axis=-1, keepdims=True) + eps_norm)
    gain_grad = jnp.sum(upstream * values * inverse, axis=0)
    scaled = upstream * gain
    inner = jnp.mean(scaled * values, axis=-1, keepdims=True)
    return (inverse * (scaled - values * inverse * inverse * inner), gain_grad)


def rotate(values, cosine, sine):
    middle = values.shape[-1] // 2
    front_part = values[..., :middle]
    back_part = values[..., middle:]
    return jnp.concatenate(
        [front_part * cosine - back_part * sine, back_part * cosine + front_part * sine], axis=-1
    )


def gelu_exact(values):
    return jax.nn.gelu(values, approximate=False)


def packing(lengths, tokens, masks, timesteps):
    seq_count = lengths.shape[0]
    position = jnp.arange(SEQ_LEN, dtype=jnp.int32)
    doc_ends = jnp.cumsum(lengths, axis=1)
    doc_starts = doc_ends - lengths
    segment = jnp.sum((position[None, :, None] >= doc_ends[:, None, :]).astype(jnp.int32), axis=2)
    chosen = segment[:, :, None] == jnp.arange(DOCS, dtype=jnp.int32)[None, None, :]
    offset = position[None, :] - jnp.sum(jnp.where(chosen, doc_starts[:, None, :], 0), axis=2)
    is_real = segment < DOCS - 1
    targets = tokens.reshape(seq_count, SEQ_LEN)
    corrupt = masks.reshape(seq_count, SEQ_LEN) == 1
    inputs = jnp.where(corrupt, VOCAB - 1, targets)
    factor = jnp.where(timesteps == 1, 1.0, T_DIFF / timesteps.astype(jnp.float32))
    weights = jnp.where(corrupt & is_real, factor[:, None], 0.0)
    inverse_freq = 10000.0 ** (-jnp.arange(HEAD_DIM // 2, dtype=jnp.float32) / (HEAD_DIM // 2))
    angles = offset.astype(jnp.float32)[:, :, None] * inverse_freq
    return (inputs, targets, weights, segment, is_real, jnp.cos(angles), jnp.sin(angles))


def scores_of(query, key_rows, segment):
    same_doc = segment[:, None] == segment[None, :]
    scores = jnp.einsum(
        "qhe,khe->hqk", query, key_rows, preferred_element_type=jnp.float32
    ) * HEAD_DIM ** (-0.5)
    return jnp.where(same_doc[None], scores, neg_fill)


def attend_one(query, key_rows, value_rows, segment):
    scores = scores_of(query, key_rows, segment)
    row_max = jnp.max(scores, axis=-1, keepdims=True)
    expd = jnp.exp(scores - row_max)
    summed = jnp.sum(expd, axis=-1, keepdims=True)
    probs = (expd / summed).astype(jnp.bfloat16)
    output = jnp.einsum("hqk,khe->qhe", probs, value_rows, preferred_element_type=jnp.float32)
    return (output.astype(jnp.bfloat16), (row_max + jnp.log(summed))[..., 0])


def attend_back(query, key_rows, value_rows, segment, row_lse, grad_out):
    scores = scores_of(query, key_rows, segment)
    probs = jnp.exp(scores - row_lse[..., None])
    value_grad = jnp.einsum(
        "hqk,qhe->khe", probs.astype(jnp.bfloat16), grad_out, preferred_element_type=jnp.float32
    )
    prob_grad = jnp.einsum("qhe,khe->hqk", grad_out, value_rows, preferred_element_type=jnp.float32)
    inner = jnp.sum(prob_grad * probs, axis=-1, keepdims=True)
    score_grad = (probs * (prob_grad - inner)).astype(jnp.bfloat16)
    query_grad = jnp.einsum(
        "hqk,khe->qhe", score_grad, key_rows, preferred_element_type=jnp.float32
    ) * HEAD_DIM ** (-0.5)
    key_grad = jnp.einsum(
        "hqk,qhe->khe", score_grad, query, preferred_element_type=jnp.float32
    ) * HEAD_DIM ** (-0.5)
    return (query_grad, key_grad, value_grad)


def vocab_stats(normed, vocab_rows, targets, vocab_start):
    logits = jnp.einsum("rd,vd->rv", normed, vocab_rows, preferred_element_type=jnp.float32)
    local_max = jnp.max(logits, axis=-1)
    local_sum = jnp.sum(jnp.exp(logits - local_max[:, None]), axis=-1)
    target_hit = (targets - vocab_start)[:, None] == jnp.arange(
        vocab_rows.shape[0], dtype=jnp.int32
    )[None, :]
    return (local_max, local_sum, jnp.sum(jnp.where(target_hit, logits, 0.0), axis=-1))


def vocab_back(normed, vocab_rows, targets, vocab_start, row_lse, row_weight):
    logits = jnp.einsum("rd,vd->rv", normed, vocab_rows, preferred_element_type=jnp.float32)
    target_hit = (
        (targets - vocab_start)[:, None]
        == jnp.arange(vocab_rows.shape[0], dtype=jnp.int32)[None, :]
    ).astype(jnp.float32)
    logit_grad = (row_weight[:, None] * (jnp.exp(logits - row_lse[:, None]) - target_hit)).astype(
        jnp.bfloat16
    )
    table_part = jnp.einsum("rv,rd->vd", logit_grad, normed, preferred_element_type=jnp.float32)
    normed_grad = jnp.einsum(
        "rv,vd->rd", logit_grad, vocab_rows, preferred_element_type=jnp.float32
    )
    return (table_part, normed_grad)


def combine(earlier, later):
    max_early, sum_early, pick_early = earlier
    max_late, sum_late, pick_late = later
    top_value = jnp.maximum(max_early, max_late)
    return (
        top_value,
        sum_early * jnp.exp(max_early - top_value) + sum_late * jnp.exp(max_late - top_value),
        pick_early + pick_late,
    )


def per_device(
    tokens,
    lengths,
    timesteps,
    masks,
    step_count,
    table,
    joint_weight,
    output_weight,
    upward_weight,
    downward_weight,
    gains,
    momentum_table,
    momentum_joint,
    momentum_output,
    momentum_upward,
    momentum_downward,
    momentum_gains,
    variance_table,
    variance_joint,
    variance_output,
    variance_upward,
    variance_downward,
    variance_gains,
):
    vocab_rows, joint_rows, output_rows, upward_rows, downward_rows, gain_rows = (
        lax.all_gather(table.astype(jnp.bfloat16), "dp", axis=1, tiled=True),
        lax.all_gather(joint_weight.astype(jnp.bfloat16), "dp", axis=0, tiled=True),
        lax.all_gather(output_weight.astype(jnp.bfloat16), "dp", axis=1, tiled=True),
        lax.all_gather(upward_weight.astype(jnp.bfloat16), "dp", axis=0, tiled=True),
        lax.all_gather(downward_weight.astype(jnp.bfloat16), "dp", axis=1, tiled=True),
        lax.all_gather(gains.astype(jnp.bfloat16), "dp", axis=1, tiled=True),
    )
    gain_full = gain_rows.astype(jnp.float32)
    inputs, targets, weights, segment, is_real, cosine, sine = packing(
        lengths, tokens, masks, timesteps
    )
    seq_count = lengths.shape[0]
    row_count = tokens.shape[0]
    vocab_local = vocab_rows.shape[0]
    vocab_start = lax.axis_index("tensor") * vocab_local
    local_ids = inputs.reshape(row_count) - vocab_start
    inside = (local_ids >= 0) & (local_ids < vocab_local)
    safe_ids = jnp.clip(local_ids, 0, vocab_local - 1)
    looked = jnp.take(vocab_rows, safe_ids, axis=0).astype(jnp.float32) * D**0.5
    embedded = tensor_total(jnp.where(inside[:, None], looked, 0.0))
    normed_one = norm_apply(embedded, gain_full[0]).astype(jnp.bfloat16)
    heads_local = joint_rows.shape[1] // (3 * HEAD_DIM)
    projected = jnp.dot(normed_one, joint_rows, preferred_element_type=jnp.float32).reshape(
        seq_count, SEQ_LEN, heads_local, 3, HEAD_DIM
    )
    rot_cos = cosine[:, :, None, :]
    rot_sin = sine[:, :, None, :]
    query = rotate(projected[:, :, :, 0], rot_cos, rot_sin).astype(jnp.bfloat16)
    key_rows = rotate(projected[:, :, :, 1], rot_cos, rot_sin).astype(jnp.bfloat16)
    value_rows = projected[:, :, :, 2].astype(jnp.bfloat16)
    attended, attn_lse = lax.map(
        lambda items: attend_one(*items), (query, key_rows, value_rows, segment)
    )
    attended_flat = attended.reshape(row_count, heads_local * HEAD_DIM)
    attn_part = jnp.dot(attended_flat, output_rows, preferred_element_type=jnp.float32)
    after_attn = embedded + tensor_total(attn_part)
    normed_two = norm_apply(after_attn, gain_full[1]).astype(jnp.bfloat16)
    pre_gelu = jnp.dot(normed_two, upward_rows, preferred_element_type=jnp.float32)
    gelu_value, gelu_pull = jax.vjp(gelu_exact, pre_gelu)
    activated = gelu_value.astype(jnp.bfloat16)
    mlp_part = jnp.dot(activated, downward_rows, preferred_element_type=jnp.float32)
    after_mlp = after_attn + tensor_total(mlp_part)
    normed_out = norm_apply(after_mlp, gain_full[2]).astype(jnp.bfloat16)
    per_seq = normed_out.reshape(seq_count, SEQ_LEN, D)
    stats = lax.map(
        lambda items: vocab_stats(items[0], vocab_rows, items[1], vocab_start), (per_seq, targets)
    )
    row_max, row_sum, row_pick = joined(
        (stats[0].reshape(row_count), stats[1].reshape(row_count), stats[2].reshape(row_count)),
        "tensor",
        combine,
    )
    row_lse = row_max + jnp.log(row_sum)
    loss_local = jnp.sum(weights.reshape(row_count) * (row_lse - row_pick))
    count_local = jnp.sum(is_real.astype(jnp.float32))
    loss_total, count_total = lax.psum((loss_local, count_local), "dp")

    def head_step(carry, items):
        normed_rows, target_rows, lse_rows, weight_rows = items
        table_part, normed_grad = vocab_back(
            normed_rows, vocab_rows, target_rows, vocab_start, lse_rows, weight_rows
        )
        return (carry + table_part, normed_grad)

    table_grad, out_grad = lax.scan(
        head_step,
        jnp.zeros(vocab_rows.shape, jnp.float32),
        (per_seq, targets, row_lse.reshape(seq_count, SEQ_LEN), weights),
    )
    out_grad = tensor_total(out_grad.reshape(row_count, D))
    mlp_grad, gain_three = norm_back(after_mlp, gain_full[2], out_grad)
    mlp_branch = mlp_grad.astype(jnp.bfloat16)
    downward_grad = jnp.einsum(
        "rf,rd->fd", activated, mlp_branch, preferred_element_type=jnp.float32
    )
    act_grad = jnp.einsum(
        "rd,fd->rf", mlp_branch, downward_rows, preferred_element_type=jnp.float32
    )
    up_input = gelu_pull(act_grad)[0].astype(jnp.bfloat16)
    upward_grad = jnp.einsum("rd,rf->df", normed_two, up_input, preferred_element_type=jnp.float32)
    normed_two_grad = tensor_total(
        jnp.einsum("rf,df->rd", up_input, upward_rows, preferred_element_type=jnp.float32)
    )
    attn_in_grad, gain_two = norm_back(after_attn, gain_full[1], normed_two_grad)
    resid_one = mlp_grad + attn_in_grad
    attn_branch = resid_one.astype(jnp.bfloat16)
    output_grad = jnp.einsum(
        "ra,rd->ad", attended_flat, attn_branch, preferred_element_type=jnp.float32
    )
    attended_grad = (
        jnp.einsum("rd,ad->ra", attn_branch, output_rows, preferred_element_type=jnp.float32)
        .astype(jnp.bfloat16)
        .reshape(seq_count, SEQ_LEN, heads_local, HEAD_DIM)
    )
    query_grad, key_grad, value_grad = lax.map(
        lambda items: attend_back(*items),
        (query, key_rows, value_rows, segment, attn_lse, attended_grad),
    )
    query_grad = rotate(query_grad, rot_cos, -rot_sin)
    key_grad = rotate(key_grad, rot_cos, -rot_sin)
    proj_grad = (
        jnp.stack([query_grad, key_grad, value_grad], axis=3)
        .reshape(row_count, heads_local * 3 * HEAD_DIM)
        .astype(jnp.bfloat16)
    )
    joint_grad = jnp.einsum("rd,rc->dc", normed_one, proj_grad, preferred_element_type=jnp.float32)
    normed_one_grad = tensor_total(
        jnp.einsum("rc,dc->rd", proj_grad, joint_rows, preferred_element_type=jnp.float32)
    )
    embed_in, gain_one = norm_back(embedded, gain_full[0], normed_one_grad)
    embed_grad = resid_one + embed_in
    gain_grad = jnp.stack([gain_one, gain_two, gain_three])
    table_grad = table_grad + jax.ops.segment_sum(
        jnp.where(inside[:, None], embed_grad * D**0.5, 0.0), safe_ids, num_segments=vocab_local
    )
    table_sum, joint_sum, output_sum, upward_sum, downward_sum, gain_sum = (
        lax.psum_scatter(table_grad, "dp", scatter_dimension=1, tiled=True),
        lax.psum_scatter(joint_grad, "dp", scatter_dimension=0, tiled=True),
        lax.psum_scatter(output_grad, "dp", scatter_dimension=1, tiled=True),
        lax.psum_scatter(upward_grad, "dp", scatter_dimension=0, tiled=True),
        lax.psum_scatter(downward_grad, "dp", scatter_dimension=1, tiled=True),
        lax.psum_scatter(gain_grad, "dp", scatter_dimension=1, tiled=True),
    )
    reduced = (table_sum, joint_sum, output_sum, upward_sum, downward_sum, gain_sum)
    local_square = jnp.zeros((), jnp.float32)
    for grad_item in reduced[:5]:
        local_square = local_square + jnp.sum(grad_item * grad_item)
    local_square = local_square + jnp.sum(gain_sum * gain_sum) / lax.axis_size("tensor")
    square_total = lax.psum(local_square, ("dp", "tensor"))
    grad_norm = jnp.sqrt(square_total) / count_total
    clip_scale = jnp.minimum(1.0, clip_at / grad_norm)
    loss = loss_total / count_total
    step_float = step_count[0].astype(jnp.float32)
    fix_one = 1.0 - jnp.power(beta_one, step_float)
    fix_two = 1.0 - jnp.power(beta_two, step_float)
    masters = (table, joint_weight, output_weight, upward_weight, downward_weight, gains)
    moments_one = (
        momentum_table,
        momentum_joint,
        momentum_output,
        momentum_upward,
        momentum_downward,
        momentum_gains,
    )
    moments_two = (
        variance_table,
        variance_joint,
        variance_output,
        variance_upward,
        variance_downward,
        variance_gains,
    )
    updated = []
    for index in range(6):
        clipped = reduced[index] / count_total * clip_scale
        moment_one = beta_one * moments_one[index] + (1.0 - beta_one) * clipped
        moment_two = beta_two * moments_two[index] + (1.0 - beta_two) * clipped * clipped
        stepped = moment_one / fix_one / (jnp.sqrt(moment_two / fix_two) + adam_eps)
        master = masters[index]
        updated.extend(
            [moment_one, moment_two, master - rates[index] * (stepped + decays[index] * master)]
        )
    return tuple([loss, grad_norm] + updated)


def solution(mesh):
    placed = (
        P("dp"),
        P("dp", None),
        P("dp"),
        P("dp"),
        P(),
        P("tensor", "dp"),
        P("dp", "tensor"),
        P("tensor", "dp"),
        P("dp", "tensor"),
        P("tensor", "dp"),
        P(None, "dp"),
        P("tensor", "dp"),
        P("dp", "tensor"),
        P("tensor", "dp"),
        P("dp", "tensor"),
        P("tensor", "dp"),
        P(None, "dp"),
        P("tensor", "dp"),
        P("dp", "tensor"),
        P("tensor", "dp"),
        P("dp", "tensor"),
        P("tensor", "dp"),
        P(None, "dp"),
    )
    return jax.shard_map(
        per_device,
        mesh=mesh,
        in_specs=placed,
        out_specs=(
            P(),
            P(),
            P("tensor", "dp"),
            P("tensor", "dp"),
            P("tensor", "dp"),
            P("dp", "tensor"),
            P("dp", "tensor"),
            P("dp", "tensor"),
            P("tensor", "dp"),
            P("tensor", "dp"),
            P("tensor", "dp"),
            P("dp", "tensor"),
            P("dp", "tensor"),
            P("dp", "tensor"),
            P("tensor", "dp"),
            P("tensor", "dp"),
            P("tensor", "dp"),
            P(None, "dp"),
            P(None, "dp"),
            P(None, "dp"),
        ),
        check_vma=False,
    )
```

profile of v0, /device:TPU:0, one launch (start us, length us, event | category | flops | bytes accessed | tf_op | source)
XLA Modules:
  0.0 1684.2 jit_solution(2242139781662490906)
XLA Ops:
  11.9 62.1 %all-gather.8.cloned.1.call-done = bf16[2048,768]{0,1:T(8,128)(2,1)} async-done(((bf16[2048,96]{0,1:T(8,128)(2,1)}), bf16[2048,768]{0,1:T(8,128)(2,1)}) %all-gather.8.cloned.1.call-update) | async-done | bytes 3145744 | tf_op jit(solution)/shard_map/all_gather | solution.py:180
  77.2 9.6 gather_fusion
  91.7 18.2 %all-gather = bf16[8,96,3]{1,2,0:T(4,128)(2,1)S(1)} all-gather(bf16[1,96,3]{1,2,0:T(4,128)(2,1)S(1)} %convert_bitcast_fusion.1), channel_id=1, replica_groups=mesh['dp'=8,'tensor'=4] {'dp'}, dimensions={0}, use_global_device_ids=true | all-gather | bytes 5184 | tf_op jit(solution)/shard_map/all_gather | solution.py:185
  111.0 33.3 %all_gather.30 = bf16[192,768]{0,1:T(8,128)(2,1)} all-gather(bf16[192,96]{0,1:T(8,128)(2,1)S(1)} %copy.126), channel_id=1, replica_groups=mesh['dp'=8,'tensor'=4] {'dp'}, dimensions={1}, use_global_device_ids=true | all-gather | bytes 331776 | tf_op jit(solution)/shard_map/all_gather | solution.py:182
  146.0 32.9 %all_gather.29 = bf16[768,576]{1,0:T(8,128)(2,1)S(1)} all-gather(bf16[96,576]{1,0:T(8,128)(2,1)S(1)} %convert_element_type.106), channel_id=1, replica_groups=mesh['dp'=8,'tensor'=4] {'dp'}, dimensions={0}, use_global_device_ids=true | all-gather | bytes 995328 | tf_op jit(solution)/shard_map/all_gather | solution.py:181
  178.9 30.9 %all-reduce.8.cloned.1.call-done = f32[2048,768]{1,0:T(8,128)} async-done(((f32[2048,768]{1,0:T(8,128)}), f32[2048,768]{1,0:T(8,128)}) %all-reduce.8.cloned.1.call-update) | async-done | bytes 6291472 | tf_op jit(solution)/shard_map/psum | solution.py:33
  218.9 7.9 reshape.255
  236.3 29.2 %while.72 = (s32[]{:T(128)}, bf16[2,1024,3,64]{1,3,2,0:T(8,128)(2,1)}, f32[2,3,1024]{2,1,0:T(4,128)S(1)}, bf16[2,1024,3,64]{1,3,2,0:T(8,128)(2,1)}, s32[2,1024]{...) while((s32[]{:T(128)}, ...), condition=%wide.region_8.9_spmd.clone, body=%wide.region_5.8_spmd.sunk.clone | while | flops 844297216 | bytes 47835256 | solution.py:210
  274.1 118.3 %all-reduce.10.cloned.1.call-done = f32[2048,768]{1,0:T(8,128)} async-done(((f32[2048,768]{1,0:T(8,128)}), f32[2048,768]{1,0:T(8,128)}) %all-reduce.10.cloned.1.call-update) | async-done | bytes 6291472 | tf_op jit(solution)/shard_map/psum | solution.py:33
  392.3 7.9 multiply_reduce_fusion.8
  400.3 36.0 %all-gather.10.cloned.1.call-done = bf16[768,768]{1,0:T(8,128)(2,1)} async-done(((bf16[96,768]{1,0:T(8,128)(2,1)}), bf16[768,768]{1,0:T(8,128)(2,1)}) %all-gather.10.cloned.1.call-update) | async-done | bytes 1179664 | tf_op jit(solution)/shard_map/all_gather | solution.py:183
  436.2 19.1 %multiply_convert_fusion.3 = (bf16[2048,768]{1,0:T(8,128)(2,1)S(1)}, f32[2048,768]{1,0:T(8,128)}, f32[2048,768]{1,0:T(8,128)}) fusion(bf16[768,768]{1,0:T(8,128)(2,1)} %all-gather.10.cloned.1.call-done, f32[2048,768]{1,0:T(8,128)} %get-tuple-element.571, f32[768]{0:T(1024)S(1)} %copy-done.60, f32[2048]{0:T(1024)S(1)} %add_rsqrt_fusion.1), kind=kOutput, calls=%fused_computation.111 | convolution fusion | flops 2522873856 | bytes 23211008 | tf_op jit(solution)/shard_map/dot_general | solution.py:217
  455.4 23.3 %all-gather.12.cloned.1.call-done = bf16[768,768]{0,1:T(8,128)(2,1)} async-done(((bf16[768,96]{0,1:T(8,128)(2,1)}), bf16[768,768]{0,1:T(8,128)(2,1)}) %all-gather.12.cloned.1.call-update) | async-done | bytes 1179664 | tf_op jit(solution)/shard_map/all_gather | solution.py:184
  485.4 117.6 %all-reduce.12.cloned.1.call-done = f32[2048,768]{1,0:T(8,128)} async-done(((f32[2048,768]{1,0:T(8,128)}), f32[2048,768]{1,0:T(8,128)}) %all-reduce.12.cloned.1.call-update) | async-done | bytes 6291472 | tf_op jit(solution)/shard_map/psum | solution.py:33
  614.0 16.7 while.73
  647.6 34.0 %while.76 = (s32[]{:T(128)}, f32[2048,768]{1,0:T(8,128)}, f32[2,1024,768]{2,1,0:T(8,128)}, f32[2,1024]{1,0:T(2,128)S(1)}, bf16[2,1024,768]{2,1,0:T(8,128)(2,1)},...) while((s32[]{:T(128)}, f32[2048,768]{1,0:T(8,128)}, ...), condition=%wide.region_25.26_spmd.clone.clone, body=%wide.region_24.25_spmd.clone.sunk.clone | while | flops 9679406080 | bytes 151032080 | solution.py:244
  681.7 119.9 %all-reduce.14.cloned.1.call-done = f32[2048,768]{1,0:T(8,128)} async-done(((f32[2048,768]{1,0:T(8,128)}), f32[2048,768]{1,0:T(8,128)}) %all-reduce.14.cloned.1.call-update) | async-done | bytes 6291472 | tf_op jit(solution)/shard_map/psum | solution.py:33
  812.3 8.2 add_convert_fusion
  826.9 119.9 %all-reduce.16.cloned.1.call-done = f32[2048,768]{1,0:T(8,128)} async-done(((f32[2048,768]{1,0:T(8,128)}), f32[2048,768]{1,0:T(8,128)}) %all-reduce.16.cloned.1.call-update) | async-done | bytes 6291472 | tf_op jit(solution)/shard_map/psum | solution.py:33
  965.6 50.4 %while.75 = (s32[]{:T(128)}, f32[2,1024,3,64]{1,3,2,0:T(8,128)}, f32[2,1024,3,64]{1,3,2,0:T(8,128)}, bf16[2,1024,3,64]{1,3,2,0:T(8,128)(2,1)}, bf16[2,1024,3,64]...) while((s32[]{:T(128)}, f32[2,1024,3,64]{1,3,2,0:T(8,128)}, ...), condition=%wide.region_32.33_spmd.clone, body=%wide.region_30.32_spmd.sunk.clone | while | flops 2061890560 | bytes 135247168 | solution.py:274
  997.1 7.1 multiply_reduce_fusion.18
  1033.0 8.1 fusion.89
  1041.5 8.0 fusion.110
  1049.6 97.2 %all-reduce.18.cloned.1.call-done = f32[2048,768]{1,0:T(8,128)} async-done(((f32[2048,768]{1,0:T(8,128)}), f32[2048,768]{1,0:T(8,128)}) %all-reduce.18.cloned.1.call-update) | async-done | bytes 6291472 | tf_op jit(solution)/shard_map/psum | solution.py:33
  1160.4 23.3 %scatter_custom_fusion = f32[2048,768]{1,0:T(8,128)} fusion(f32[2048,768]{1,0:T(8,128)} %get-tuple-element.250, s32[2048]{0:T(1024)} %copy-done.65, f32[2048,768]{1,0:T(8,128)} %copy-done.5, f32[2048,768]{1,0:T(8,128)} %all-reduce.18.cloned.1.call-done, f32[2048,768]{1,0:T(8,128)} %all-reduce.8.cloned.1.call-done, f32[2048]{0:T(1024)S(1)} %broadcast_multiply_fusion, ...), kind=kCustom, calls=%fused_computation.95 | custom fusion | flops 15728640 | bytes 25188352 | tf_op jit(solution)/shard_map/scatter-add | solution.py:292
  1191.9 22.5 %all-reduce = (f32[]{:T(128)}, f32[]{:T(128)}) all-reduce(f32[]{:T(128)} %get-tuple-element.564, f32[]{:T(128)} %convert_reduce_fusion.1), channel_id=1, replica_groups=mesh['dp'=8,'tensor'=4] {'dp'}, use_global_device_ids=true, to_apply=%region_21.22 | all-reduce | flops 2 | bytes 16 | tf_op jit(solution)/shard_map/psum | solution.py:235
  1216.8 68.4 %reduce-scatter.17.cloned.1.call-done = f32[768,96]{0,1:T(8,128)} async-done(((f32[768,768]{0,1:T(8,128)}), f32[768,96]{0,1:T(8,128)}) %reduce-scatter.17.cloned.1.call-update) | async-done | bytes 294928 | tf_op jit(solution)/shard_map/reduce_scatter | solution.py:300
  1286.9 70.1 %reduce-scatter.15.cloned.1.call-done = f32[96,768]{1,0:T(8,128)} async-done(((f32[768,768]{1,0:T(8,128)}), f32[96,768]{1,0:T(8,128)}) %reduce-scatter.15.cloned.1.call-update) | async-done | bytes 294928 | tf_op jit(solution)/shard_map/reduce_scatter | solution.py:299
  1358.6 63.0 %reduce-scatter.23.cloned.1.call-done = f32[96,3]{1,0:T(8,128)} async-done(((f32[768,3]{1,0:T(8,128)}), f32[96,3]{1,0:T(8,128)}) %reduce-scatter.23.cloned.1.call-update) | async-done | bytes 1168
  1423.8 67.4 %reduce-scatter.13.cloned.1.call-done = f32[96,576]{1,0:T(8,128)} async-done(((f32[768,576]{1,0:T(8,128)}), f32[96,576]{1,0:T(8,128)}) %reduce-scatter.13.cloned.1.call-update) | async-done | bytes 221200 | tf_op jit(solution)/shard_map/reduce_scatter | solution.py:297
  1492.8 118.7 %reduce-scatter.19.cloned.1.call-done = f32[96,2048]{1,0:T(8,128)} async-done(((f32[768,2048]{1,0:T(8,128)}), f32[96,2048]{1,0:T(8,128)}) %reduce-scatter.19.cloned.1.call-update) | async-done | bytes 786448
  1618.6 39.7 %psum.71 = f32[]{:T(128)} all-reduce(f32[]{:T(128)S(6)} %add.255), channel_id=1, replica_groups=mesh['dp'=8,'tensor'=4] {'dp','tensor'}, use_global_device_ids=true, to_apply=%region_51.52 | all-reduce | flops 1 | bytes 8 | tf_op jit(solution)/shard_map/psum | solution.py:308
  (402 shorter events, 298.5 us)
Async XLA Ops:
  7.2 66.8 %all-gather.8.cloned.1.call-start = ((), (), s32[]{:S(2)}) async-start(), calls=%async_computation.6 | async-start | bytes 3538944 | tf_op jit(solution)/shard_map/all_gather | solution.py:180
  9.2 200.6 %all-reduce.8.cloned.1.call-start = ((), (), s32[]{:S(2)}) async-start(), calls=%async_computation.7 | async-start | bytes 12582912 | tf_op jit(solution)/shard_map/psum | solution.py:33
  91.4 300.9 %all-reduce.10.cloned.1.call-start = ((), (), s32[]{:S(2)}) async-start(), calls=%async_computation.8 | async-start | bytes 12582912 | tf_op jit(solution)/shard_map/psum | solution.py:33
  110.9 108.1 %copy-start.52 = (f32[768]{0:T(1024)}, f32[768]{0:T(1024)S(1)}, u32[]{:S(2)}) copy-start(f32[768]{0:T(1024)S(1)} %get-tuple-element.457) | copy-start | bytes 9220
  265.6 219.7 %copy-start.43 = (s32[2,1024]{1,0:T(2,128)}, s32[2,1024]{1,0:T(2,128)S(1)}, u32[]{:S(2)}) copy-start(s32[2,1024]{1,0:T(2,128)S(1)} %get-tuple-element.1178) | copy-start | bytes 24580
  272.4 163.9 %all-gather.10.cloned.1.call-start = ((), (), s32[]{:S(2)}) async-start(), calls=%async_computation.9 | async-start | bytes 1327104 | tf_op jit(solution)/shard_map/all_gather | solution.py:183
  273.1 205.6 %all-gather.12.cloned.1.call-start = ((), (), s32[]{:S(2)}) async-start(), calls=%async_computation.10 | async-start | bytes 1327104 | tf_op jit(solution)/shard_map/all_gather | solution.py:184
  274.0 162.2 %copy-start.60 = (f32[768]{0:T(1024)S(1)}, f32[768]{0:T(1024)}, u32[]{:S(2)}) copy-start(f32[768]{0:T(1024)} %get-tuple-element.456) | copy-start | bytes 9220
  274.0 329.0 %all-reduce.12.cloned.1.call-start = ((), (), s32[]{:S(2)}) async-start(), calls=%async_computation.11 | async-start | bytes 12582912 | tf_op jit(solution)/shard_map/psum | solution.py:33
  484.5 317.1 %all-reduce.14.cloned.1.call-start = ((), (), s32[]{:S(2)}) async-start(), calls=%async_computation.12 | async-start | bytes 12582912 | tf_op jit(solution)/shard_map/psum | solution.py:33
  485.4 123.0 %copy-start.63 = (pred[2,1024]{1,0:T(4,128)(4,1)}, pred[2,1024]{1,0:T(4,128)(4,1)S(1)}, u32[]{:S(2)}) copy-start(pred[2,1024]{1,0:T(4,128)(4,1)S(1)} %get-tuple-element.563) | copy-start | bytes 6148
  485.4 126.2 %copy-start.58 = (f32[768]{0:T(1024)S(1)}, f32[768]{0:T(1024)}, u32[]{:S(2)}) copy-start(f32[768]{0:T(1024)} %get-tuple-element.455) | copy-start | bytes 9220
  681.6 120.0 %copy-start.51 = (f32[2048]{0:T(1024)S(1)}, f32[2048]{0:T(1024)}, u32[]{:S(2)}) copy-start(f32[2048]{0:T(1024)} %copy-done.50) | copy-start | bytes 24580
  681.6 120.0 %copy-start.59 = (f32[768]{0:T(1024)S(1)}, f32[768]{0:T(1024)}, u32[]{:S(2)}) copy-start(f32[768]{0:T(1024)} %get-tuple-element.455) | copy-start | bytes 9220
  681.6 265.2 %all-reduce.16.cloned.1.call-start = ((), (), s32[]{:S(2)}) async-start(), calls=%async_computation.13 | async-start | bytes 12582912 | tf_op jit(solution)/shard_map/psum | solution.py:33
  826.8 120.0 %copy-start.56 = (f32[2048]{0:T(1024)S(1)}, f32[2048]{0:T(1024)}, u32[]{:S(2)}) copy-start(f32[2048]{0:T(1024)} %copy-done.55) | copy-start | bytes 24580
  826.8 120.0 %copy-start.61 = (f32[768]{0:T(1024)S(1)}, f32[768]{0:T(1024)}, u32[]{:S(2)}) copy-start(f32[768]{0:T(1024)} %get-tuple-element.456) | copy-start | bytes 9220
  826.9 319.9 %all-reduce.18.cloned.1.call-start = ((), (), s32[]{:S(2)}) async-start(), calls=%async_computation.14 | async-start | bytes 12582912 | tf_op jit(solution)/shard_map/psum | solution.py:33
  1026.8 188.3 %reduce-scatter.21.cloned.1.call-start = ((), (), s32[]{:S(2)}) async-start(), calls=%async_computation.19 | async-start | bytes 884736
  1033.0 252.2 %reduce-scatter.17.cloned.1.call-start = ((), (), s32[]{:S(2)}) async-start(), calls=%async_computation.17 | async-start | bytes 2654208 | tf_op jit(solution)/shard_map/reduce_scatter | solution.py:300
  1041.2 315.8 %reduce-scatter.15.cloned.1.call-start = ((), (), s32[]{:S(2)}) async-start(), calls=%async_computation.16 | async-start | bytes 2654208 | tf_op jit(solution)/shard_map/reduce_scatter | solution.py:299
  1049.5 372.1 %reduce-scatter.23.cloned.1.call-start = ((), (), s32[]{:S(2)}) async-start(), calls=%async_computation.20 | async-start | bytes 442368
  1153.2 338.0 %reduce-scatter.13.cloned.1.call-start = ((), (), s32[]{:S(2)}) async-start(), calls=%async_computation.15 | async-start | bytes 2211840 | tf_op jit(solution)/shard_map/reduce_scatter | solution.py:297
  1160.4 451.2 %reduce-scatter.19.cloned.1.call-start = ((), (), s32[]{:S(2)}) async-start(), calls=%async_computation.18 | async-start | bytes 7077888
  1190.4 469.5 %copy-start.73 = (f32[3,96]{1,0:T(4,128)S(1)}, f32[3,96]{1,0:T(4,128)}, u32[]{:S(2)}) copy-start(f32[3,96]{1,0:T(4,128)} %param.43) | copy-start | bytes 3460
  1190.4 469.5 %copy-start.75 = (f32[3,96]{1,0:T(4,128)S(1)}, f32[3,96]{1,0:T(4,128)}, u32[]{:S(2)}) copy-start(f32[3,96]{1,0:T(4,128)} %param.55) | copy-start | bytes 3460
  1190.4 469.5 %copy-start.76 = (f32[3,96]{1,0:T(4,128)S(1)}, f32[3,96]{1,0:T(4,128)}, u32[]{:S(2)}) copy-start(f32[3,96]{1,0:T(4,128)} %param.49) | copy-start | bytes 3460
  1190.4 476.3 %copy-start.32 = (f32[768,96]{0,1:T(8,128)S(1)}, f32[768,96]{0,1:T(8,128)}, u32[]{:S(2)}) copy-start(f32[768,96]{0,1:T(8,128)} %param.42) | copy-start | bytes 884740
  1190.4 479.1 %copy-start.34 = (f32[96,768]{1,0:T(8,128)S(1)}, f32[96,768]{1,0:T(8,128)}, u32[]{:S(2)}) copy-start(f32[96,768]{1,0:T(8,128)} %param.41) | copy-start | bytes 884740
  1190.4 481.9 %copy-start.24 = (f32[2048,96]{0,1:T(8,128)S(1)}, f32[2048,96]{0,1:T(8,128)}, u32[]{:S(2)}) copy-start(f32[2048,96]{0,1:T(8,128)} %param.38) | copy-start | bytes 2359300
  1216.1 395.4 %copy-start.37 = (f32[192,96]{1,0:T(8,128)}, f32[192,96]{1,0:T(8,128)S(1)}, u32[]{:S(2)}) copy-start(f32[192,96]{1,0:T(8,128)S(1)} %copy.139) | copy-start | bytes 221188
  1285.2 381.5 %copy-start.35 = (f32[768,96]{0,1:T(8,128)S(1)}, f32[768,96]{0,1:T(8,128)}, u32[]{:S(2)}) copy-start(f32[768,96]{0,1:T(8,128)} %reduce-scatter.17.cloned.1.call-done) | copy-start | bytes 884740
  (79 other events, 1047.9 us)
Sparse Core Ops, SparseCore 0:
  10.8 63.1 all-gather.7
  91.6 118.1 all-reduce.7
  272.5 119.7 all-reduce.9
  394.9 41.2 all-gather.9
  438.8 39.8 all-gather.11
  484.7 118.3 all-reduce.11
  681.7 119.8 all-reduce.13
  827.0 119.7 all-reduce.15
  1027.0 119.7 all-reduce.17
  1150.5 62.6 reduce-scatter.20
  1217.1 68.0 reduce-scatter.16
  1289.0 68.0 reduce-scatter.14
  1361.2 60.4 reduce-scatter.22
  1425.4 65.7 reduce-scatter.12
  1494.7 116.8 reduce-scatter.18
where the time goes:
time: 1690 us; the launch traced here: 1680 us
  waiting for transfers between devices  1110 us (66%)
  matrix products  170 us (10%)
  blocking collectives  162 us (10%)
  other arithmetic  141 us (8%)
  local copies, waits for them, and re-layouts  69.6 us (4%)
  between operations  26 us (2%)
    psum x6, waiting for transfers between devices, tensor_total(): return lax.psum(partial_value, 'tensor')  604 us
    unnamed x18, waiting for transfers between devices  182 us
    reduce_scatter x1, waiting for transfers between devices, per_device(): lax.psum_scatter(upward_grad, 'dp', scatter_dimension=0, tiled=True)  70.1 us
    reduce_scatter x1, waiting for transfers between devices, per_device(): lax.psum_scatter(downward_grad, 'dp', scatter_dimension=1, tiled=True)  68.4 us
    reduce_scatter x1, waiting for transfers between devices, per_device(): lax.psum_scatter(joint_grad, 'dp', scatter_dimension=0, tiled=True)  67.4 us
    all_gather x1, waiting for transfers between devices, per_device(): lax.all_gather(table.astype(jnp.bfloat16), 'dp', axis=1, tiled=True)  62.1 us
    psum x1, blocking collectives, per_device(): square_total = lax.psum(local_square, ('dp', 'tensor'))  39.7 us
    all_gather x1, waiting for transfers between devices, per_device(): lax.all_gather(upward_weight.astype(jnp.bfloat16), 'dp', axis=0, tiled=True)  36 us
  transfers between devices with their start and end apart: 15, of which 14 were waited for; matrix products, arithmetic and copies ran while one was open for 6% of the time, Pallas kernels for 0%

commit v1 on v0

v1 whole, which is shorter than its diff:
```python
import jax
import jax.numpy as jnp
from jax import lax
from jax.sharding import PartitionSpec as P

D = 768
HEAD_DIM = 64
VOCAB = 8192
SEQ_LEN = 1024
DOCS = 4
T_DIFF = 1000


eps_norm = 1e-06
neg_fill = -1000000000.0
beta_one = 0.9
beta_two = 0.999
adam_eps = 1e-08
clip_at = 0.02
rates = (0.05, 0.03, 0.25, 0.03, 0.03, 0.3)
decays = (0.1, 0.1, 0.1, 0.1, 0.1, 0.0)


def norm_apply(values, gain):
    inverse = lax.rsqrt(jnp.mean(values * values, axis=-1, keepdims=True) + eps_norm)
    return values * inverse * gain


def norm_back(values, gain, upstream):
    inverse = lax.rsqrt(jnp.mean(values * values, axis=-1, keepdims=True) + eps_norm)
    gain_grad = jnp.sum(upstream * values * inverse, axis=0)
    scaled = upstream * gain
    inner = jnp.mean(scaled * values, axis=-1, keepdims=True)
    return (inverse * (scaled - values * inverse * inverse * inner), gain_grad)


def rotate(values, cosine, sine):
    middle = values.shape[-1] // 2
    front_part = values[..., :middle]
    back_part = values[..., middle:]
    return jnp.concatenate(
        [front_part * cosine - back_part * sine, back_part * cosine + front_part * sine], axis=-1
    )


def groups_of(count):
    groups, bit, width = [], 1, 1
    while bit < count:
        masks = [bit]
        if width == 2 and bit * 2 < count:
            masks = [bit, 2 * bit, 3 * bit]
            bit = bit * 2
        groups.append(masks)
        bit, width = bit * 2, 2
    return groups


def swap(value, axis, mask):
    size = lax.axis_size(axis)
    return lax.ppermute(value, axis, [(place, place ^ mask) for place in range(size)])


def spread(value, masks):
    return jnp.concatenate([value] + [swap(value, "dp", mask) for mask in masks], axis=0)


def gather_all(value, x_last):
    groups = groups_of(lax.axis_size("dp"))
    for masks in groups[:0:-1]:
        value = spread(value, masks)
    if x_last:
        value = spread(value, groups[0])
        other = swap(value, "tensor", 2)
    else:
        other = swap(value, "tensor", 2)
        value = spread(value, groups[0])
        other = spread(other, groups[0])
    return [value, other, swap(value, "tensor", 1), swap(other, "tensor", 1)]


def wide(value):
    return value.astype(jnp.float32)


def narrow(value):
    return value.astype(jnp.bfloat16)


def fold(value, masks, last):
    rows = value.shape[0] // (len(masks) + 1)
    total = wide(value[:rows])
    for place, mask in enumerate(masks):
        total = total + wide(swap(value[(place + 1) * rows : (place + 2) * rows], "dp", mask))
    return total if last else narrow(total)


def reduce_all(quarters, x_first):
    groups = groups_of(lax.axis_size("dp"))
    own = narrow(wide(quarters[0]) + wide(swap(quarters[2], "tensor", 1)))
    other = narrow(wide(quarters[1]) + wide(swap(quarters[3], "tensor", 1)))
    if x_first:
        own = narrow(wide(own) + wide(swap(other, "tensor", 2)))
        own = fold(own, groups[0], len(groups) == 1)
    else:
        own = fold(own, groups[0], False)
        other = fold(other, groups[0], False)
        own = narrow(wide(own) + wide(swap(other, "tensor", 2)))
    for place in range(1, len(groups)):
        own = fold(own, groups[place], place == len(groups) - 1)
    return wide(own)


def everyone_sum(value):
    for masks in groups_of(lax.axis_size("dp")):
        value = sum([swap(value, "dp", mask) for mask in masks], value)
    for mask in (1, 2):
        value = value + swap(value, "tensor", mask)
    return value


def mm(left, right):
    return jnp.dot(left, right, preferred_element_type=jnp.float32)


def mm_nt(left, right):
    return lax.dot_general(left, right, (((1,), (1,)), ((), ())), preferred_element_type=jnp.float32)


def mm_tn(left, right):
    return lax.dot_general(left, right, (((0,), (0,)), ((), ())), preferred_element_type=jnp.float32)


def gelu_exact(values):
    return jax.nn.gelu(values, approximate=False)


def rotate_heads(values, cosine, sine):
    return rotate(values, cosine[:, None, :], sine[:, None, :])


def scores_of(query, key_rows, same_doc):
    scores = jnp.einsum(
        "qhe,khe->hqk", query, key_rows, preferred_element_type=jnp.float32
    ) * HEAD_DIM ** (-0.5)
    return jnp.where(same_doc[None], scores, neg_fill)


def split_heads(packed):
    packed = packed.reshape(packed.shape[0], -1, 3, HEAD_DIM)
    return packed[:, :, 0], packed[:, :, 1], packed[:, :, 2]


def attend(packed, same_doc):
    query, key_rows, value_rows = split_heads(packed)
    scores = scores_of(query, key_rows, same_doc)
    row_max = jnp.max(scores, axis=-1, keepdims=True)
    expd = jnp.exp(scores - row_max)
    summed = jnp.sum(expd, axis=-1, keepdims=True)
    probs = (expd / summed).astype(jnp.bfloat16)
    output = jnp.einsum("hqk,khe->qhe", probs, value_rows, preferred_element_type=jnp.float32)
    return (narrow(output).reshape(packed.shape[0], -1), (row_max + jnp.log(summed))[..., 0])


def attend_back(packed, same_doc, row_lse, grad_out, cosine, sine):
    query, key_rows, value_rows = split_heads(packed)
    grad_out = grad_out.reshape(packed.shape[0], -1, HEAD_DIM)
    scores = scores_of(query, key_rows, same_doc)
    probs = jnp.exp(scores - row_lse[..., None])
    value_grad = jnp.einsum(
        "hqk,qhe->khe", probs.astype(jnp.bfloat16), grad_out, preferred_element_type=jnp.float32
    )
    prob_grad = jnp.einsum("qhe,khe->hqk", grad_out, value_rows, preferred_element_type=jnp.float32)
    inner = jnp.sum(prob_grad * probs, axis=-1, keepdims=True)
    score_grad = (probs * (prob_grad - inner)).astype(jnp.bfloat16)
    query_grad = jnp.einsum(
        "hqk,khe->qhe", score_grad, key_rows, preferred_element_type=jnp.float32
    ) * HEAD_DIM ** (-0.5)
    key_grad = jnp.einsum(
        "hqk,qhe->khe", score_grad, query, preferred_element_type=jnp.float32
    ) * HEAD_DIM ** (-0.5)
    query_grad = rotate_heads(query_grad, cosine, -sine)
    key_grad = rotate_heads(key_grad, cosine, -sine)
    return narrow(jnp.stack([query_grad, key_grad, value_grad], axis=2).reshape(packed.shape))


def per_device(
    tokens,
    lengths,
    timesteps,
    masks,
    step_count,
    table,
    joint_weight,
    output_weight,
    upward_weight,
    downward_weight,
    gains,
    momentum_table,
    momentum_joint,
    momentum_output,
    momentum_upward,
    momentum_downward,
    momentum_gains,
    variance_table,
    variance_joint,
    variance_output,
    variance_upward,
    variance_downward,
    variance_gains,
):
    place = lax.axis_index("tensor")
    parts = lax.axis_size("tensor")
    rows = tokens.shape[0] // parts
    vocab_part, head_part = table.shape[0], joint_weight.shape[1]
    out_part, ff_part = output_weight.shape[0], upward_weight.shape[1]
    half_vocab = vocab_part // 2

    table_t = narrow(table).T
    left_half = gather_all(table_t[:, :half_vocab], True)
    right_half = gather_all(table_t[:, half_vocab:], False)
    gain_columns = jnp.pad(narrow(gains).T, ((0, 0), (0, 61)))
    first_group = gather_all(jnp.concatenate([narrow(joint_weight), gain_columns], axis=1), True)
    second_group = gather_all(
        jnp.concatenate(
            [narrow(upward_weight), narrow(downward_weight).T, narrow(output_weight).T], axis=1
        ),
        True,
    )
    table_q = [piece for pair in zip(left_half, right_half) for piece in pair]
    joint_q = [item[:, :head_part] for item in first_group]
    gain_full = wide(first_group[0][:, head_part : head_part + 3]).T
    up_q = [item[:, :ff_part] for item in second_group]
    down_q = [item[:, ff_part : 2 * ff_part] for item in second_group]
    out_all = jnp.concatenate([item[:, 2 * ff_part :] for item in second_group], axis=1)

    start = place * rows
    seq = start // SEQ_LEN
    mine = start - seq * SEQ_LEN
    cut = lambda array: lax.dynamic_slice(array, (start,), (rows,))
    targets = cut(tokens)
    corrupt = cut(masks) == 1
    inputs = jnp.where(corrupt, VOCAB - 1, targets)
    own_lengths = lax.dynamic_slice(lengths, (seq, 0), (1, DOCS))
    step_here = lax.dynamic_slice(timesteps, (seq,), (1,))
    theirs = mine ^ rows
    position = jnp.concatenate(
        [mine + jnp.arange(rows, dtype=jnp.int32), theirs + jnp.arange(rows, dtype=jnp.int32)]
    )
    doc_ends = jnp.cumsum(own_lengths[0])
    doc_starts = doc_ends - own_lengths[0]
    segment = jnp.sum((position[:, None] >= doc_ends[None, :]).astype(jnp.int32), axis=1)
    chosen = segment[:, None] == jnp.arange(DOCS, dtype=jnp.int32)[None, :]
    offset = position - jnp.sum(jnp.where(chosen, doc_starts[None, :], 0), axis=1)
    is_real = segment < DOCS - 1
    factor = jnp.where(step_here == 1, 1.0, T_DIFF / step_here.astype(jnp.float32))
    weights = jnp.where(corrupt & is_real[:rows], factor, 0.0)
    inverse_freq = 10000.0 ** (-jnp.arange(HEAD_DIM // 2, dtype=jnp.float32) / (HEAD_DIM // 2))
    angles = offset.astype(jnp.float32)[:, None] * inverse_freq
    cosine, sine = jnp.cos(angles), jnp.sin(angles)
    same_doc = segment[:, None] == segment[None, :]

    def hot(ids, piece):
        quarter, side = piece // 2, piece % 2
        owner = place ^ (2 * (quarter % 2) + quarter // 2)
        base = owner * vocab_part + side * half_vocab
        return (ids - base)[:, None] == jnp.arange(half_vocab, dtype=jnp.int32)[None, :]

    pieces = range(len(table_q))
    input_hot = [narrow(hot(inputs, piece)) for piece in pieces]
    looked = sum(mm_nt(input_hot[piece], table_q[piece]) for piece in pieces)
    embedded = looked * D**0.5
    normed_one = narrow(norm_apply(embedded, gain_full[0]))

    def turned(projected):
        projected = projected.reshape(rows, -1, 3, HEAD_DIM)
        query = rotate_heads(projected[:, :, 0], cosine[:rows], sine[:rows])
        key_rows = rotate_heads(projected[:, :, 1], cosine[:rows], sine[:rows])
        stacked = jnp.stack([query, key_rows, projected[:, :, 2]], axis=2)
        return narrow(stacked.reshape(rows, -1))

    packed = [turned(mm(normed_one, item)) for item in joint_q]
    whole = [
        jnp.concatenate([packed[side], swap(packed[2 + side], "tensor", 1)], axis=0)
        for side in range(2)
    ]
    attended, attn_lse = zip(*[attend(item, same_doc) for item in whole])
    attended_all = jnp.concatenate(
        [item[:rows] for item in attended]
        + [swap(item[rows:], "tensor", 1) for item in attended],
        axis=1,
    )
    after_attn = embedded + mm_nt(attended_all, out_all)
    normed_two = narrow(norm_apply(after_attn, gain_full[1]))
    pre_gelu = [mm(normed_two, item) for item in up_q]
    gelu_pairs = [jax.vjp(gelu_exact, item) for item in pre_gelu]
    activated = [narrow(item[0]) for item in gelu_pairs]
    after_mlp = after_attn + sum(mm_nt(activated[q], down_q[q]) for q in range(4))
    normed_out = narrow(norm_apply(after_mlp, gain_full[2]))
    logits = [mm(normed_out, item) for item in table_q]
    row_max = logits[0].max(axis=1)
    for item in logits[1:]:
        row_max = jnp.maximum(row_max, item.max(axis=1))
    row_sum = sum(jnp.sum(jnp.exp(item - row_max[:, None]), axis=1) for item in logits)
    target_hot = [hot(targets, piece) for piece in pieces]
    row_pick = sum(
        jnp.sum(jnp.where(target_hot[piece], logits[piece], 0.0), axis=1) for piece in pieces
    )
    row_lse = row_max + jnp.log(row_sum)
    loss_local = jnp.sum(weights * (row_lse - row_pick))
    count_local = jnp.sum(is_real[:rows].astype(jnp.float32))

    logit_grad = [
        narrow(
            weights[:, None]
            * (jnp.exp(logits[piece] - row_lse[:, None]) - target_hot[piece].astype(jnp.float32))
        )
        for piece in pieces
    ]
    out_grad = sum(mm_nt(logit_grad[piece], table_q[piece]) for piece in pieces)
    mlp_grad, gain_three = norm_back(after_mlp, gain_full[2], out_grad)
    mlp_branch = narrow(mlp_grad)
    down_grad = [narrow(mm_tn(mlp_branch, item)) for item in activated]
    down_sum = reduce_all(down_grad, True)
    up_input = [
        narrow(gelu_pairs[q][1](mm(mlp_branch, down_q[q]))[0]) for q in range(4)
    ]
    up_grad = [narrow(mm_tn(normed_two, item)) for item in up_input]
    up_sum = reduce_all(up_grad, False)
    normed_two_grad = sum(mm_nt(up_input[q], up_q[q]) for q in range(4))
    attn_in_grad, gain_two = norm_back(after_attn, gain_full[1], normed_two_grad)
    resid_one = mlp_grad + attn_in_grad
    attn_branch = narrow(resid_one)
    out_grads = narrow(mm_tn(attn_branch, attended_all))
    out_sum = reduce_all(
        [out_grads[:, q * out_part : (q + 1) * out_part] for q in range(4)], False
    )
    attended_grad = narrow(mm(attn_branch, out_all))
    grad_parts = [attended_grad[:, q * out_part : (q + 1) * out_part] for q in range(4)]
    proj_whole = [
        attend_back(
            whole[side],
            same_doc,
            attn_lse[side],
            jnp.concatenate(
                [grad_parts[side], swap(grad_parts[2 + side], "tensor", 1)], axis=0
            ),
            cosine,
            sine,
        )
        for side in range(2)
    ]
    proj_grad = [item[:rows] for item in proj_whole] + [
        swap(item[rows:], "tensor", 1) for item in proj_whole
    ]
    normed_one_grad = sum(mm_nt(proj_grad[q], joint_q[q]) for q in range(4))
    embed_in, gain_one = norm_back(embedded, gain_full[0], normed_one_grad)
    embed_grad = resid_one + embed_in
    gain_grad = jnp.pad(narrow(jnp.stack([gain_one, gain_two, gain_three])).T, ((0, 0), (0, 61)))
    joint_grad = [
        jnp.concatenate([narrow(mm_tn(normed_one, item)), gain_grad], axis=1) for item in proj_grad
    ]
    joint_sum = reduce_all(joint_grad, True)
    embed_scaled = narrow(embed_grad * D**0.5)
    table_grad = [
        narrow(mm_tn(normed_out, logit_grad[piece]) + mm_tn(embed_scaled, input_hot[piece]))
        for piece in pieces
    ]
    table_left = reduce_all(table_grad[0::2], True)
    table_right = reduce_all(table_grad[1::2], False)
    gain_sum = joint_sum[:, head_part : head_part + 3].T
    reduced = (
        jnp.concatenate([table_left, table_right], axis=1).T,
        joint_sum[:, :head_part],
        out_sum.T,
        up_sum,
        down_sum.T,
        gain_sum,
    )
    local_square = jnp.zeros((), jnp.float32)
    for grad_item in reduced[:5]:
        local_square = local_square + jnp.sum(grad_item * grad_item)
    local_square = local_square + jnp.sum(gain_sum * gain_sum) / parts
    totals = everyone_sum(jnp.stack([local_square, loss_local, count_local]))
    square_total, loss_total, count_total = totals[0], totals[1], totals[2]
    grad_norm = jnp.sqrt(square_total) / count_total
    clip_scale = jnp.minimum(1.0, clip_at / grad_norm)
    loss = loss_total / count_total
    step_float = step_count[0].astype(jnp.float32)
    fix_one = 1.0 - jnp.power(beta_one, step_float)
    fix_two = 1.0 - jnp.power(beta_two, step_float)
    masters = (table, joint_weight, output_weight, upward_weight, downward_weight, gains)
    moments_one = (
        momentum_table,
        momentum_joint,
        momentum_output,
        momentum_upward,
        momentum_downward,
        momentum_gains,
    )
    moments_two = (
        variance_table,
        variance_joint,
        variance_output,
        variance_upward,
        variance_downward,
        variance_gains,
    )
    updated = []
    for index in range(6):
        clipped = reduced[index] / count_total * clip_scale
        moment_one = beta_one * moments_one[index] + (1.0 - beta_one) * clipped
        moment_two = beta_two * moments_two[index] + (1.0 - beta_two) * clipped * clipped
        stepped = moment_one / fix_one / (jnp.sqrt(moment_two / fix_two) + adam_eps)
        master = masters[index]
        updated.extend(
            [moment_one, moment_two, master - rates[index] * (stepped + decays[index] * master)]
        )
    return tuple([loss, grad_norm] + updated)


def solution(mesh):
    placed = (
        P("dp"),
        P("dp", None),
        P("dp"),
        P("dp"),
        P(),
        P("tensor", "dp"),
        P("dp", "tensor"),
        P("tensor", "dp"),
        P("dp", "tensor"),
        P("tensor", "dp"),
        P(None, "dp"),
        P("tensor", "dp"),
        P("dp", "tensor"),
        P("tensor", "dp"),
        P("dp", "tensor"),
        P("tensor", "dp"),
        P(None, "dp"),
        P("tensor", "dp"),
        P("dp", "tensor"),
        P("tensor", "dp"),
        P("dp", "tensor"),
        P("tensor", "dp"),
        P(None, "dp"),
    )
    return jax.shard_map(
        per_device,
        mesh=mesh,
        in_specs=placed,
        out_specs=(
            P(),
            P(),
            P("tensor", "dp"),
            P("tensor", "dp"),
            P("tensor", "dp"),
            P("dp", "tensor"),
            P("dp", "tensor"),
            P("dp", "tensor"),
            P("tensor", "dp"),
            P("tensor", "dp"),
            P("tensor", "dp"),
            P("dp", "tensor"),
            P("dp", "tensor"),
            P("dp", "tensor"),
            P("tensor", "dp"),
            P("tensor", "dp"),
            P("tensor", "dp"),
            P(None, "dp"),
            P(None, "dp"),
            P(None, "dp"),
        ),
        check_vma=False,
    )
```

time: 1690 us -> 694 us (0.41)
  waiting for transfers between devices: 1110 us -> 219 us
  blocking collectives: 162 us -> 0 us
  starting transfers between devices: 0.88 us -> 93.5 us
  other arithmetic: 141 us -> 73.2 us
  matrix products: 170 us -> 205 us
    psum x6 -> x0, waiting for transfers between devices: 604 us -> none  [tensor_total(): return lax.psum(partial_value, 'tensor')]
    ppermute x0 -> x88, waiting for transfers between devices: none -> 219 us  [swap(): lax.ppermute(value, axis, [(place, place ^ mask) for place in range(size)])]
    reduce_scatter x3 -> x0, waiting for transfers between devices: 206 us -> none  [the longest x1 70.1 us: per_device(): lax.psum_scatter(upward_grad, 'dp', scatter_dimension=0, tiled=True)]
    unnamed x18 -> x0, waiting for transfers between devices: 182 us -> none
    all_gather x3 -> x0, waiting for transfers between devices: 121 us -> none  [the longest x1 62.1 us: per_device(): lax.all_gather(table.astype(jnp.bfloat16), 'dp', axis=1, tiled=True)]
    all_gather x6 -> x0, blocking collectives: 99.9 us -> none  [the longest x1 33.3 us: per_device(): lax.all_gather(output_weight.astype(jnp.bfloat16), 'dp', axis=1, tiled=True)]
    ppermute x0 -> x88, starting transfers between devices: none -> 93.5 us  [swap(): lax.ppermute(value, axis, [(place, place ^ mask) for place in range(size)])]
    psum x2 -> x0, blocking collectives: 62.2 us -> none  [the longest x1 39.7 us: per_device(): square_total = lax.psum(local_square, ('dp', 'tensor'))]
  transfers between devices with their start and end apart: 15 -> 88, of which waited for: 14 -> 32; matrix products, arithmetic and copies ran while one was open for 6% -> 30% of each run, Pallas kernels for 0% -> 0%
where the time goes in v1:
time: 694 us; the launch traced here: 685 us
  waiting for transfers between devices  219 us (32%)
  matrix products  205 us (30%)
  starting transfers between devices  93.5 us (13%)
  local copies, waits for them, and re-layouts  78.8 us (11%)
  other arithmetic  73.2 us (11%)
  between operations  16.1 us (2%)
    ppermute x88, waiting for transfers between devices, swap(): lax.ppermute(value, axis, [(place, place ^ mask) for place in range(size)])  219 us
    ppermute x88, starting transfers between devices, swap(): lax.ppermute(value, axis, [(place, place ^ mask) for place in range(size)])  93.5 us
    dot_general x29, matrix products, mm_nt(): lax.dot_general(left, right, (((1,), (1,)), ((), ())), preferred_element_...  57.5 us
    dot_general x21, matrix products, mm(): return jnp.dot(left, right, preferred_element_type=jnp.float32)  55.6 us
    dot_general x29, matrix products, mm_tn(): lax.dot_general(left, right, (((0,), (0,)), ((), ())), preferred_element_...  45 us
    unnamed x418, local copies, waits for them, and re-layouts  41.4 us
  transfers between devices with their start and end apart: 88, of which 32 were waited for; matrix products, arithmetic and copies ran while one was open for 30% of the time, Pallas kernels for 0%

profile of v1, /device:TPU:0, one launch (start us, length us, event | category | flops | bytes accessed | tf_op | source)
XLA Modules:
  0.0 685.2 jit_solution(947663531749554430)
XLA Ops:
  9.8 3.9 collective-permute-start.17
  43.0 8.3 %collective-permute-done.6 = bf16[96,1024]{1,0:T(8,128)(2,1)S(1)} collective-permute-done((bf16[96,1024]{1,0:T(8,128)(2,1)S(1)}, bf16[96,1024]{1,0:T(8,128)(2,1)S(1)}, u32[]{:S(2)}, u32[]{:S(2)}) %collective-permute-start.6) | collective-permute-done | bytes 196640 | tf_op jit(solution)/shard_map/ppermute | solution.py:60
  51.5 17.0 %collective-permute-done.5 = bf16[96,1024]{1,0:T(8,128)(2,1)S(1)} collective-permute-done((bf16[96,1024]{1,0:T(8,128)(2,1)S(1)}, bf16[96,1024]{1,0:T(8,128)(2,1)S(1)}, u32[]{:S(2)}, u32[]{:S(2)}) %collective-permute-start.5) | collective-permute-done | bytes 196640 | tf_op jit(solution)/shard_map/ppermute | solution.py:60
  75.2 4.3 collective-permute-done.27
  95.9 9.1 %collective-permute-done.7 = bf16[384,1024]{1,0:T(8,128)(2,1)} collective-permute-done((bf16[384,1024]{1,0:T(8,128)(2,1)}, bf16[384,1024]{1,0:T(8,128)(2,1)}, u32[]{:S(2)}, u32[]{:S(2)}) %collective-permute-start.7) | collective-permute-done | bytes 786464 | tf_op jit(solution)/shard_map/ppermute | solution.py:60
  110.3 32.6 %collective-permute-done.10 = bf16[384,1024]{1,0:T(8,128)(2,1)S(1)} collective-permute-done((bf16[384,1024]{1,0:T(8,128)(2,1)}, bf16[384,1024]{1,0:T(8,128)(2,1)S(1)}, u32[]{:S(2)}, u32[]{:S(2)}) %collective-permute-start.10) | collective-permute-done | bytes 786464 | tf_op jit(solution)/shard_map/ppermute | solution.py:60
  150.4 5.8 concatenate.147
  183.2 43.1 %collective-permute-done.30 = bf16[768,1728]{0,1:T(8,128)(2,1)} collective-permute-done((bf16[768,1728]{0,1:T(8,128)(2,1)S(1)}, bf16[768,1728]{0,1:T(8,128)(2,1)}, u32[]{:S(2)}, u32[]{:S(2)}) %collective-permute-start.30) | collective-permute-done | bytes 2654240 | tf_op jit(solution)/shard_map/ppermute | solution.py:60
  254.9 5.4 multiply_convert_fusion.15
  261.2 6.5 multiply_convert_fusion.12
  267.7 5.4 multiply_convert_fusion.13
  273.1 6.6 multiply_convert_fusion.14
  307.5 5.7 select_reduce_fusion.6
  369.5 7.7 %fusion.65 = bf16[1024,3,1,64]{0,3,1,2:T(8,128)(2,1)} fusion(bf16[1024,3,64]{0,2,1:T(8,128)(2,1)} %bitcast.319, f32[3,1024,1024]{1,2,0:T(8,128)} %copy-done.1, f32[3,1024]{1,0:T(4,128)} %log_add_fusion), kind=kOutput, calls=%fused_computation.222 | convolution fusion | flops 409141248 | bytes 13381632 | tf_op jit(solution)/shard_map/hqk,qhe->khe/dot_general | solution.py:169
  377.2 6.3 multiply_reduce_fusion
  384.4 5.3 multiply_convert_fusion
  389.7 5.0 fusion.54
  401.6 6.3 multiply_reduce_fusion.1
  409.9 5.7 multiply_convert_fusion.1
  415.6 5.0 fusion.55
  492.0 12.5 %collective-permute-done.70 = bf16[384,768]{1,0:T(8,128)(2,1)S(1)} collective-permute-done((bf16[384,768]{1,0:T(8,128)(2,1)S(1)}, bf16[384,768]{1,0:T(8,128)(2,1)S(1)}, u32[]{:S(2)}, u32[]{:S(2)}) %collective-permute-start.70) | collective-permute-done | bytes 589856 | tf_op jit(solution)/shard_map/ppermute | solution.py:60
  506.1 8.8 %collective-permute-done.77 = bf16[768,768]{1,0:T(8,128)(2,1)S(1)} collective-permute-done((bf16[768,768]{1,0:T(8,128)(2,1)S(1)}, bf16[768,768]{1,0:T(8,128)(2,1)S(1)}, u32[]{:S(2)}, u32[]{:S(2)}) %collective-permute-start.77) | collective-permute-done | bytes 1179680 | tf_op jit(solution)/shard_map/ppermute | solution.py:60
  519.2 11.9 %collective-permute-done.71 = bf16[384,768]{1,0:T(8,128)(2,1)S(1)} collective-permute-done((bf16[384,768]{1,0:T(8,128)(2,1)S(1)}, bf16[384,768]{1,0:T(8,128)(2,1)S(1)}, u32[]{:S(2)}, u32[]{:S(2)}) %collective-permute-start.71) | collective-permute-done | bytes 589856 | tf_op jit(solution)/shard_map/ppermute | solution.py:60
  536.4 6.8 collective-permute-done.78
  571.3 7.9 %collective-permute-done.55 = bf16[384,640]{0,1:T(8,128)(2,1)S(1)} collective-permute-done((bf16[384,640]{0,1:T(8,128)(2,1)S(1)}, bf16[384,640]{0,1:T(8,128)(2,1)S(1)}, u32[]{:S(2)}, u32[]{:S(2)}) %collective-permute-start.55) | collective-permute-done | bytes 491552 | tf_op jit(solution)/shard_map/ppermute | solution.py:60
  581.8 6.3 collective-permute-done.39
  597.2 4.0 collective-permute-done.48
  607.7 4.0 collective-permute-done.40
  614.9 10.6 %collective-permute-start.41 = (bf16[96,1024]{1,0:T(8,128)(2,1)S(1)}, bf16[96,1024]{1,0:T(8,128)(2,1)S(1)}, u32[]{:S(2)}, u32[]{:S(2)}) collective-permute-start(bf16[96,1024]{1,0:T(8,128)(2,1)S(1)} %get-tuple-element.204), channel_id=1, source_target_pairs={{0,8},{4,12},{8,0},{12,4},{16,24},{20,28},{24,16},{28,20},{1,9},{5... | collective-permute-start | bytes 589832 | tf_op jit(solution)/shard_map/ppermute | solution.py:60
  625.5 4.9 collective-permute-done.50
  630.4 7.3 %collective-permute-done.42 = bf16[96,1024]{1,0:T(8,128)(2,1)S(1)} collective-permute-done((bf16[96,1024]{1,0:T(8,128)(2,1)S(1)}, bf16[96,1024]{1,0:T(8,128)(2,1)S(1)}, u32[]{:S(2)}, u32[]{:S(2)}) %collective-permute-start.42) | collective-permute-done | bytes 196640 | tf_op jit(solution)/shard_map/ppermute | solution.py:60
  671.8 4.0 multiply_subtract_fusion
  (823 shorter events, 385.1 us)
Async XLA Ops:
  2.8 34.0 %collective-permute-start = (bf16[96,1024]{1,0:T(8,128)(2,1)S(1)}, bf16[96,1024]{1,0:T(8,128)(2,1)S(1)}, u32[]{:S(2)}, u32[]{:S(2)}) collective-permute-start(bf16[96,1024]{1,0:T(8,128)(2,1)S(1)} %get-tuple-element.243), channel_id=1, source_target_pairs={{0,8},{4,12},{8,0},{12,4},{16,24},{20,28},{24,16},{28,20},{1,9},{5... | collective-permute-start | bytes 589832 | tf_op jit(solution)/shard_map/ppermute | solution.py:60
  5.8 31.4 %collective-permute-start.1 = (bf16[96,1024]{1,0:T(8,128)(2,1)S(1)}, bf16[96,1024]{1,0:T(8,128)(2,1)S(1)}, u32[]{:S(2)}, u32[]{:S(2)}) collective-permute-start(bf16[96,1024]{1,0:T(8,128)(2,1)S(1)} %get-tuple-element.243), channel_id=1, source_target_pairs={{0,16},{4,20},{8,24},{12,28},{16,0},{20,4},{24,8},{28,12},{1,17},{... | collective-permute-start | bytes 589832 | tf_op jit(solution)/shard_map/ppermute | solution.py:60
  31.0 42.7 %collective-permute-start.26 = (bf16[96,1728]{1,0:T(8,128)(2,1)S(1)}, bf16[96,1728]{1,0:T(8,128)(2,1)S(1)}, u32[]{:S(2)}, u32[]{:S(2)}) collective-permute-start(bf16[96,1728]{1,0:T(8,128)(2,1)S(1)} %pad_maximum_fusion.17), channel_id=1, source_target_pairs={{0,8},{4,12},{8,0},{12,4},{16,24},{20,28},{24,16},{28,20},{1,9},{5... | collective-permute-start | bytes 995336 | tf_op jit(solution)/shard_map/ppermute | solution.py:60
  36.7 31.7 %collective-permute-start.5 = (bf16[96,1024]{1,0:T(8,128)(2,1)S(1)}, bf16[96,1024]{1,0:T(8,128)(2,1)S(1)}, u32[]{:S(2)}, u32[]{:S(2)}) collective-permute-start(bf16[96,1024]{1,0:T(8,128)(2,1)S(1)} %get-tuple-element.246), channel_id=1, source_target_pairs={{0,16},{4,20},{8,24},{12,28},{16,0},{20,4},{24,8},{28,12},{1,17},{... | collective-permute-start | bytes 589832 | tf_op jit(solution)/shard_map/ppermute | solution.py:60
  37.2 32.0 %collective-permute-start.4 = (bf16[96,1024]{1,0:T(8,128)(2,1)S(1)}, bf16[96,1024]{1,0:T(8,128)(2,1)S(1)}, u32[]{:S(2)}, u32[]{:S(2)}) collective-permute-start(bf16[96,1024]{1,0:T(8,128)(2,1)S(1)} %get-tuple-element.246), channel_id=1, source_target_pairs={{0,8},{4,12},{8,0},{12,4},{16,24},{20,28},{24,16},{28,20},{1,9},{5... | collective-permute-start | bytes 589832 | tf_op jit(solution)/shard_map/ppermute | solution.py:60
  40.6 43.4 %collective-permute-start.3 = (bf16[384,1024]{1,0:T(8,128)(2,1)}, bf16[384,1024]{1,0:T(8,128)(2,1)}, u32[]{:S(2)}, u32[]{:S(2)}) collective-permute-start(bf16[384,1024]{1,0:T(8,128)(2,1)} %pad_maximum_fusion.6), channel_id=1, source_target_pairs={{0,4},{4,0},{8,12},{12,8},{16,20},{20,16},{24,28},{28,24},{1,5},{5... | collective-permute-start | bytes 2359304 | tf_op jit(solution)/shard_map/ppermute | solution.py:60
  51.3 28.2 %collective-permute-start.27 = (bf16[96,1728]{1,0:T(8,128)(2,1)S(1)}, bf16[96,1728]{1,0:T(8,128)(2,1)S(1)}, u32[]{:S(2)}, u32[]{:S(2)}) collective-permute-start(bf16[96,1728]{1,0:T(8,128)(2,1)S(1)} %pad_maximum_fusion.17), channel_id=1, source_target_pairs={{0,16},{4,20},{8,24},{12,28},{16,0},{20,4},{24,8},{28,12},{1,17},{... | collective-permute-start | bytes 995336 | tf_op jit(solution)/shard_map/ppermute | solution.py:60
  83.5 60.3 %collective-permute-start.29 = (bf16[384,1728]{0,1:T(8,128)(2,1)}, bf16[384,1728]{0,1:T(8,128)(2,1)}, u32[]{:S(2)}, u32[]{:S(2)}) collective-permute-start(bf16[384,1728]{0,1:T(8,128)(2,1)} %copy.235), channel_id=1, source_target_pairs={{0,4},{4,0},{8,12},{12,8},{16,20},{20,16},{24,28},{28,24},{1,5},{5... | collective-permute-start | bytes 3981320 | tf_op jit(solution)/shard_map/ppermute | solution.py:60
  86.1 62.0 %collective-permute-start.8 = (bf16[768,1024]{1,0:T(8,128)(2,1)}, bf16[768,1024]{1,0:T(8,128)(2,1)}, u32[]{:S(2)}, u32[]{:S(2)}) collective-permute-start(bf16[768,1024]{1,0:T(8,128)(2,1)} %constant_dynamic-update-slice_fusion), channel_id=1, source_target_pairs={{0,2},{1,3},{2,0},{3,1},{4,6},{5,7},{6,4},{7,5},{8,10},{9,11},{10,... | collective-permute-start | bytes 4718600 | tf_op jit(solution)/shard_map/ppermute | solution.py:60
  89.0 53.9 %collective-permute-start.10 = (bf16[384,1024]{1,0:T(8,128)(2,1)}, bf16[384,1024]{1,0:T(8,128)(2,1)S(1)}, u32[]{:S(2)}, u32[]{:S(2)}) collective-permute-start(bf16[384,1024]{1,0:T(8,128)(2,1)} %collective-permute-done.9), channel_id=1, source_target_pairs={{0,4},{4,0},{8,12},{12,8},{16,20},{20,16},{24,28},{28,24},{1,5},{5... | collective-permute-start | bytes 2359304 | tf_op jit(solution)/shard_map/ppermute | solution.py:60
  95.2 67.7 %collective-permute-start.21 = (bf16[768,640]{1,0:T(8,128)(2,1)S(1)}, bf16[768,640]{1,0:T(8,128)(2,1)S(1)}, u32[]{:S(2)}, u32[]{:S(2)}) collective-permute-start(bf16[768,640]{1,0:T(8,128)(2,1)S(1)} %constant_dynamic-update-slice_fusion.12), channel_id=1, source_target_pairs={{0,2},{1,3},{2,0},{3,1},{4,6},{5,7},{6,4},{7,5},{8,10},{9,11},{10,... | collective-permute-start | bytes 2949128 | tf_op jit(solution)/shard_map/ppermute | solution.py:60
  107.1 56.4 %collective-permute-start.12 = (bf16[768,1024]{1,0:T(8,128)(2,1)}, bf16[768,1024]{1,0:T(8,128)(2,1)}, u32[]{:S(2)}, u32[]{:S(2)}) collective-permute-start(bf16[768,1024]{1,0:T(8,128)(2,1)} %constant_dynamic-update-slice_fusion.5), channel_id=1, source_target_pairs={{0,1},{1,0},{2,3},{3,2},{4,5},{5,4},{6,7},{7,6},{8,9},{9,8},{10,11... | collective-permute-start | bytes 4718600 | tf_op jit(solution)/shard_map/ppermute | solution.py:60
  166.2 60.1 %collective-permute-start.30 = (bf16[768,1728]{0,1:T(8,128)(2,1)S(1)}, bf16[768,1728]{0,1:T(8,128)(2,1)}, u32[]{:S(2)}, u32[]{:S(2)}) collective-permute-start(bf16[768,1728]{0,1:T(8,128)(2,1)S(1)} %copy-done.23), channel_id=1, source_target_pairs={{0,2},{1,3},{2,0},{3,1},{4,6},{5,7},{6,4},{7,5},{8,10},{9,11},{10,... | collective-permute-start | bytes 7962632 | tf_op jit(solution)/shard_map/ppermute | solution.py:60
  170.3 57.7 %collective-permute-start.31 = (bf16[768,1728]{0,1:T(8,128)(2,1)S(1)}, bf16[768,1728]{0,1:T(8,128)(2,1)S(1)}, u32[]{:S(2)}, u32[]{:S(2)}) collective-permute-start(bf16[768,1728]{0,1:T(8,128)(2,1)S(1)} %copy-done.23), channel_id=1, source_target_pairs={{0,1},{1,0},{2,3},{3,2},{4,5},{5,4},{6,7},{7,6},{8,9},{9,8},{10,11... | collective-permute-start | bytes 7962632 | tf_op jit(solution)/shard_map/ppermute | solution.py:60
  179.2 49.5 %collective-permute-start.23 = (bf16[512,576]{0,1:T(8,128)(2,1)S(1)}, bf16[512,576]{0,1:T(8,128)(2,1)S(1)}, u32[]{:S(2)}, u32[]{:S(2)}) collective-permute-start(bf16[512,576]{0,1:T(8,128)(2,1)S(1)} %bitcast.343), channel_id=1, source_target_pairs={{0,1},{1,0},{2,3},{3,2},{4,5},{5,4},{6,7},{7,6},{8,9},{9,8},{10,11... | collective-permute-start | bytes 1769480 | tf_op jit(solution)/shard_map/ppermute | solution.py:60
  182.9 57.4 %collective-permute-start.20 = (bf16[512,576]{0,1:T(8,128)(2,1)}, bf16[512,576]{0,1:T(8,128)(2,1)}, u32[]{:S(2)}, u32[]{:S(2)}) collective-permute-start(bf16[512,576]{0,1:T(8,128)(2,1)} %bitcast.20), channel_id=1, source_target_pairs={{0,1},{1,0},{2,3},{3,2},{4,5},{5,4},{6,7},{7,6},{8,9},{9,8},{10,11... | collective-permute-start | bytes 1769480 | tf_op jit(solution)/shard_map/ppermute | solution.py:60
  361.3 36.3 %collective-permute-start.33 = (bf16[512,192]{1,0:T(8,128)(2,1)}, bf16[512,192]{1,0:T(8,128)(2,1)}, u32[]{:S(2)}, u32[]{:S(2)}) collective-permute-start(bf16[512,192]{1,0:T(8,128)(2,1)} %get-tuple-element.212), channel_id=1, source_target_pairs={{0,1},{1,0},{2,3},{3,2},{4,5},{5,4},{6,7},{7,6},{8,9},{9,8},{10,11... | collective-permute-start | bytes 589832 | tf_op jit(solution)/shard_map/ppermute | solution.py:60
  364.3 64.4 %collective-permute-start.59 = (bf16[768,192]{0,1:T(8,128)(2,1)}, bf16[768,192]{0,1:T(8,128)(2,1)}, u32[]{:S(2)}, u32[]{:S(2)}) collective-permute-start(bf16[768,192]{0,1:T(8,128)(2,1)} %get-tuple-element.182), channel_id=1, source_target_pairs={{0,1},{1,0},{2,3},{3,2},{4,5},{5,4},{6,7},{7,6},{8,9},{9,8},{10,11... | collective-permute-start | bytes 884744 | tf_op jit(solution)/shard_map/ppermute | solution.py:60
  364.8 63.9 %collective-permute-start.61 = (bf16[768,192]{0,1:T(8,128)(2,1)}, bf16[768,192]{0,1:T(8,128)(2,1)}, u32[]{:S(2)}, u32[]{:S(2)}) collective-permute-start(bf16[768,192]{0,1:T(8,128)(2,1)} %get-tuple-element.183), channel_id=1, source_target_pairs={{0,1},{1,0},{2,3},{3,2},{4,5},{5,4},{6,7},{7,6},{8,9},{9,8},{10,11... | collective-permute-start | bytes 884744 | tf_op jit(solution)/shard_map/ppermute | solution.py:60
  448.5 34.9 %collective-permute-start.69 = (bf16[768,768]{1,0:T(8,128)(2,1)S(1)}, bf16[768,768]{1,0:T(8,128)(2,1)S(1)}, u32[]{:S(2)}, u32[]{:S(2)}) collective-permute-start(bf16[768,768]{1,0:T(8,128)(2,1)S(1)} %copy-done.168), channel_id=1, source_target_pairs={{0,1},{1,0},{2,3},{3,2},{4,5},{5,4},{6,7},{7,6},{8,9},{9,8},{10,11... | collective-permute-start | bytes 3538952 | tf_op jit(solution)/shard_map/ppermute | solution.py:60
  449.5 37.2 %collective-permute-start.67 = (bf16[768,768]{1,0:T(8,128)(2,1)S(1)}, bf16[768,768]{1,0:T(8,128)(2,1)S(1)}, u32[]{:S(2)}, u32[]{:S(2)}) collective-permute-start(bf16[768,768]{1,0:T(8,128)(2,1)S(1)} %copy-done.167), channel_id=1, source_target_pairs={{0,1},{1,0},{2,3},{3,2},{4,5},{5,4},{6,7},{7,6},{8,9},{9,8},{10,11... | collective-permute-start | bytes 3538952 | tf_op jit(solution)/shard_map/ppermute | solution.py:60
  449.6 35.9 %collective-permute-start.76 = (bf16[768,768]{1,0:T(8,128)(2,1)S(1)}, bf16[768,768]{1,0:T(8,128)(2,1)S(1)}, u32[]{:S(2)}, u32[]{:S(2)}) collective-permute-start(bf16[768,768]{1,0:T(8,128)(2,1)S(1)} %copy-done.166), channel_id=1, source_target_pairs={{0,1},{1,0},{2,3},{3,2},{4,5},{5,4},{6,7},{7,6},{8,9},{9,8},{10,11... | collective-permute-start | bytes 3538952 | tf_op jit(solution)/shard_map/ppermute | solution.py:60
  450.8 38.4 %collective-permute-start.75 = (bf16[768,768]{1,0:T(8,128)(2,1)S(1)}, bf16[768,768]{1,0:T(8,128)(2,1)S(1)}, u32[]{:S(2)}, u32[]{:S(2)}) collective-permute-start(bf16[768,768]{1,0:T(8,128)(2,1)S(1)} %copy-done.169), channel_id=1, source_target_pairs={{0,1},{1,0},{2,3},{3,2},{4,5},{5,4},{6,7},{7,6},{8,9},{9,8},{10,11... | collective-permute-start | bytes 3538952 | tf_op jit(solution)/shard_map/ppermute | solution.py:60
  472.0 44.8 %collective-permute-start.46 = (bf16[768,1024]{1,0:T(8,128)(2,1)S(1)}, bf16[768,1024]{1,0:T(8,128)(2,1)S(1)}, u32[]{:S(2)}, u32[]{:S(2)}) collective-permute-start(bf16[768,1024]{1,0:T(8,128)(2,1)S(1)} %add_convert_fusion.1), channel_id=1, source_target_pairs={{0,1},{1,0},{2,3},{3,2},{4,5},{5,4},{6,7},{7,6},{8,9},{9,8},{10,11... | collective-permute-start | bytes 4718600 | tf_op jit(solution)/shard_map/ppermute | solution.py:60
  485.5 60.4 %collective-permute-start.44 = (bf16[768,1024]{1,0:T(8,128)(2,1)S(1)}, bf16[768,1024]{1,0:T(8,128)(2,1)S(1)}, u32[]{:S(2)}, u32[]{:S(2)}) collective-permute-start(bf16[768,1024]{1,0:T(8,128)(2,1)S(1)} %add_convert_fusion.4), channel_id=1, source_target_pairs={{0,1},{1,0},{2,3},{3,2},{4,5},{5,4},{6,7},{7,6},{8,9},{9,8},{10,11... | collective-permute-start | bytes 4718600 | tf_op jit(solution)/shard_map/ppermute | solution.py:60
  486.8 28.1 %collective-permute-start.77 = (bf16[768,768]{1,0:T(8,128)(2,1)S(1)}, bf16[768,768]{1,0:T(8,128)(2,1)S(1)}, u32[]{:S(2)}, u32[]{:S(2)}) collective-permute-start(bf16[768,768]{1,0:T(8,128)(2,1)S(1)} %add_convert_fusion.14), channel_id=1, source_target_pairs={{0,2},{1,3},{2,0},{3,1},{4,6},{5,7},{6,4},{7,5},{8,10},{9,11},{10,... | collective-permute-start | bytes 3538952 | tf_op jit(solution)/shard_map/ppermute | solution.py:60
  491.6 41.4 %collective-permute-start.38 = (bf16[768,1024]{1,0:T(8,128)(2,1)S(1)}, bf16[768,1024]{1,0:T(8,128)(2,1)S(1)}, u32[]{:S(2)}, u32[]{:S(2)}) collective-permute-start(bf16[768,1024]{1,0:T(8,128)(2,1)S(1)} %add_convert_fusion.8), channel_id=1, source_target_pairs={{0,1},{1,0},{2,3},{3,2},{4,5},{5,4},{6,7},{7,6},{8,9},{9,8},{10,11... | collective-permute-start | bytes 4718600 | tf_op jit(solution)/shard_map/ppermute | solution.py:60
  518.7 38.2 %collective-permute-start.54 = (bf16[768,640]{0,1:T(8,128)(2,1)S(1)}, bf16[768,640]{0,1:T(8,128)(2,1)S(1)}, u32[]{:S(2)}, u32[]{:S(2)}) collective-permute-start(bf16[768,640]{0,1:T(8,128)(2,1)S(1)} %add_convert_fusion.19), channel_id=1, source_target_pairs={{0,2},{1,3},{2,0},{3,1},{4,6},{5,7},{6,4},{7,5},{8,10},{9,11},{10,... | collective-permute-start | bytes 2949128 | tf_op jit(solution)/shard_map/ppermute | solution.py:60
  545.9 35.9 %collective-permute-start.37 = (bf16[768,1024]{1,0:T(8,128)(2,1)S(1)}, bf16[768,1024]{1,0:T(8,128)(2,1)S(1)}, u32[]{:S(2)}, u32[]{:S(2)}) collective-permute-start(bf16[768,1024]{1,0:T(8,128)(2,1)S(1)} %add_convert_fusion.11), channel_id=1, source_target_pairs={{0,1},{1,0},{2,3},{3,2},{4,5},{5,4},{6,7},{7,6},{8,9},{9,8},{10,11... | collective-permute-start | bytes 4718600 | tf_op jit(solution)/shard_map/ppermute | solution.py:60
  550.8 37.3 %collective-permute-start.39 = (bf16[768,1024]{1,0:T(8,128)(2,1)S(1)}, bf16[768,1024]{1,0:T(8,128)(2,1)S(1)}, u32[]{:S(2)}, u32[]{:S(2)}) collective-permute-start(bf16[768,1024]{1,0:T(8,128)(2,1)S(1)} %add_convert_fusion.7), channel_id=1, source_target_pairs={{0,2},{1,3},{2,0},{3,1},{4,6},{5,7},{6,4},{7,5},{8,10},{9,11},{10,... | collective-permute-start | bytes 4718600 | tf_op jit(solution)/shard_map/ppermute | solution.py:60
  567.1 30.1 %collective-permute-start.45 = (bf16[384,1024]{1,0:T(8,128)(2,1)}, bf16[384,1024]{1,0:T(8,128)(2,1)}, u32[]{:S(2)}, u32[]{:S(2)}) collective-permute-start(bf16[384,1024]{1,0:T(8,128)(2,1)} %slice.665), channel_id=1, source_target_pairs={{0,4},{4,0},{8,12},{12,8},{16,20},{20,16},{24,28},{28,24},{1,5},{5... | collective-permute-start | bytes 2359304 | tf_op jit(solution)/shard_map/ppermute | solution.py:60
  570.1 31.1 %collective-permute-start.48 = (bf16[384,1024]{1,0:T(8,128)(2,1)}, bf16[384,1024]{1,0:T(8,128)(2,1)}, u32[]{:S(2)}, u32[]{:S(2)}) collective-permute-start(bf16[384,1024]{1,0:T(8,128)(2,1)} %add_convert_fusion.22), channel_id=1, source_target_pairs={{0,2},{1,3},{2,0},{3,1},{4,6},{5,7},{6,4},{7,5},{8,10},{9,11},{10,... | collective-permute-start | bytes 2359304 | tf_op jit(solution)/shard_map/ppermute | solution.py:60
  (253 other events, 2692.6 us)

commit v2 on v1

--- a/solution.py
+++ b/solution.py
@@ -1,6 +1,10 @@
+import functools
+
 import jax
 import jax.numpy as jnp
 from jax import lax
+from jax.experimental import pallas as pl
+from jax.experimental.pallas import tpu as pltpu
 from jax.sharding import PartitionSpec as P
 
 D = 768
@@ -76,6 +80,449 @@
         value = spread(value, groups[0])
         other = spread(other, groups[0])
     return [value, other, swap(value, "tensor", 1), swap(other, "tensor", 1)]
+
+
+MESH = pl.DeviceIdType.MESH
+
+
+def neighbours():
+    column, row = lax.axis_index("dp"), lax.axis_index("tensor")
+    return {
+        "x": (column, (row + 2) % 4),
+        "c": (column, row + 1 - 2 * (row % 2)),
+        "y": (column + 1 - 2 * (column % 2), row),
+        "up": (column + 2, row),
+        "down": (column - 2, row),
+    }
+
+
+def meet(z, devices):
+    barrier = pltpu.get_barrier_semaphore()
+
+    def greet(name):
+        pl.semaphore_signal(barrier, inc=1, device_id=devices[name], device_id_type=MESH)
+
+    for name in ("x", "c", "y"):
+        greet(name)
+    pl.when(z < 3)(lambda: greet("up"))
+    pl.when(z > 0)(lambda: greet("down"))
+    pl.semaphore_wait(barrier, 3 + (z + 2) // 3 + (5 - z) // 3)
+
+
+def gather_body(items, *refs):
+    ins = refs[:items]
+    outs = [refs[items + 4 * item : items + 4 * item + 4] for item in range(items)]
+    side_sem, z_sem, recv_sem, own_sem = refs[5 * items :]
+    column = lax.axis_index("dp")
+    z = column // 2
+    devices = neighbours()
+    meet(z, devices)
+    shard = [item.shape[0] for item in ins]
+    piece = [item // 2 for item in shard]
+
+    def mirror(source):
+        return source + 1 - 2 * (source % 2)
+
+    def view(item, part, quarter, source):
+        start = pl.multiple_of(source * shard[item] + part * piece[item], 8)
+        return outs[item][quarter].at[pl.ds(start, piece[item])]
+
+    def copy(item, part, quarter, source, to_quarter, name, send, own=False):
+        here = view(item, part, quarter, source)
+        if own:
+            here = ins[item].at[pl.ds(part * piece[item], piece[item])]
+        return pltpu.make_async_remote_copy(
+            src_ref=here,
+            dst_ref=view(item, part, to_quarter, source),
+            send_sem=send,
+            recv_sem=recv_sem.at[item, part, to_quarter, source],
+            device_id=devices[name],
+            device_id_type=MESH,
+        )
+
+    def arrived(item, part, quarter, source):
+        copy(item, part, quarter, source, quarter, "x", side_sem.at[0, item]).wait_recv()
+
+    def send_x(item, part, source, own=False):
+        copy(item, part, 0, source, 2, "x", side_sem.at[0, item], own).start()
+
+    def send_y(item, part, quarter, source, own=False):
+        copy(item, part, quarter, source, quarter, "y", side_sem.at[1, item], own).start()
+
+    def send_c(item, part, quarter, source, own=False):
+        copy(item, part, quarter, source, quarter + 1, "c", side_sem.at[2 + quarter // 2, item], own).start()
+
+    def send_z(item, part, source, turn, upward, own=False):
+        name = "up" if upward else "down"
+        copy(item, part, 0, source, 0, name, z_sem.at[item, part, 1 - upward, turn], own).start()
+
+    def slot(turn, action):
+        pl.when(z >= turn)(lambda: action(column - 2 * turn, 1))
+        pl.when(z + turn <= 3)(lambda: action(column + 2 * turn, 0))
+
+    every = [(item, part) for item in range(items) for part in range(2)]
+    local = [
+        pltpu.make_async_copy(
+            ins[item],
+            outs[item][0].at[pl.ds(pl.multiple_of(column * shard[item], 8), shard[item])],
+            own_sem.at[item],
+        )
+        for item in range(items)
+    ]
+    for item, part in every:
+        pl.when(z < 3)(lambda: send_z(item, part, column, 0, 1, True))
+        pl.when(z > 0)(lambda: send_z(item, part, column, 0, 0, True))
+        send_x(item, part, column, True)
+        send_y(item, part, 0, column, True)
+        send_c(item, part, 0, column, True)
+    for copied in local:
+        copied.start()
+
+    def from_z(item, part, turn, source, upward):
+        arrived(item, part, 0, source)
+        if turn < 3:
+            ahead = z < 3 if upward else z > 0
+            pl.when(ahead)(lambda: send_z(item, part, source, turn, upward))
+        send_x(item, part, source)
+        send_y(item, part, 0, source)
+        send_c(item, part, 0, source)
+
+    def second(item, source):
+        arrived(item, 0, 0, mirror(source))
+        send_x(item, 0, mirror(source))
+        send_c(item, 0, 0, mirror(source))
+        arrived(item, 1, 2, source)
+        send_y(item, 1, 2, source)
+        send_c(item, 1, 2, source)
+
+    def third(item, source):
+        arrived(item, 0, 2, source)
+        send_c(item, 0, 2, source)
+        arrived(item, 1, 0, mirror(source))
+        send_c(item, 1, 0, mirror(source))
+        for part in range(2):
+            arrived(item, part, 2, mirror(source))
+            send_c(item, part, 2, mirror(source))
+
+    for item in range(items):
+        for turn in (1, 2, 3):
+            for part in range(2):
+                slot(turn, lambda source, upward: from_z(item, part, turn, source, upward))
+    for item in range(items):
+        second(item, column)
+        for turn in (1, 2, 3):
+            slot(turn, lambda source, upward: second(item, source))
+    for item in range(items):
+        third(item, column)
+        for turn in (1, 2, 3):
+            slot(turn, lambda source, upward: third(item, source))
+    for item, part in every:
+        for source in range(8):
+            for quarter in (1, 3):
+                arrived(item, part, quarter, source)
+    for copied in local:
+        copied.wait()
+    for item in range(items):
+        for way, count in enumerate((12, 12, 16, 16)):
+            lead = outs[item][0].at[pl.ds(0, count * piece[item])]
+            pltpu.make_async_remote_copy(
+                src_ref=lead,
+                dst_ref=lead,
+                send_sem=side_sem.at[way, item],
+                recv_sem=recv_sem.at[item, 0, 0, 0],
+                device_id=devices["x"],
+                device_id_type=MESH,
+            ).wait_send()
+    for item, part in every:
+        for turn in range(3):
+            pl.when((z < 3) & (z >= turn))(
+                lambda: copy(item, part, 0, column, 0, "up", z_sem.at[item, part, 0, turn], True).wait_send()
+            )
+            pl.when((z > 0) & (z + turn <= 3))(
+                lambda: copy(item, part, 0, column, 0, "down", z_sem.at[item, part, 1, turn], True).wait_send()
+            )
+
+
+def gather_kernel(shards):
+    items = len(shards)
+    anywhere = pl.BlockSpec(memory_space=pl.ANY)
+    whole = lax.axis_size("dp")
+    shapes = [
+        jax.ShapeDtypeStruct((item.shape[0] * whole, item.shape[1]), item.dtype)
+        for item in shards
+        for _ in range(4)
+    ]
+    flat = pl.pallas_call(
+        functools.partial(gather_body, items),
+        name="gather_weights",
+        out_shape=shapes,
+        in_specs=[anywhere] * items,
+        out_specs=[anywhere] * (4 * items),
+        scratch_shapes=[
+            pltpu.SemaphoreType.DMA((4, items)),
+            pltpu.SemaphoreType.DMA((items, 2, 2, 3)),
+            pltpu.SemaphoreType.DMA((items, 2, 4, 8)),
+            pltpu.SemaphoreType.DMA((items,)),
+        ],
+        compiler_params=pltpu.CompilerParams(collective_id=0, has_side_effects=True),
+    )(*shards)
+    return [flat[4 * item : 4 * item + 4] for item in range(items)]
+
+
+def reduce_body(items, *refs):
+    ins = [refs[4 * item : 4 * item + 4] for item in range(items)]
+    outs = refs[4 * items : 5 * items]
+    held = [refs[5 * items + 7 * item : 5 * items + 7 * item + 7] for item in range(items)]
+    load_sem, side_sem, c_sem, x_sem, y_sem, zs_sem, zr_sem = refs[12 * items :]
+    column = lax.axis_index("dp")
+    z, y = column // 2, column % 2
+    devices = neighbours()
+    shard = [item.shape[0] for item in outs]
+    piece = [item // 2 for item in shard]
+
+    loads = []
+    for item in range(items):
+        for side in range(2):
+            load = pltpu.make_async_copy(
+                ins[item][2 * side], held[item][0].at[side], load_sem.at[item, side]
+            )
+            load.start()
+            loads.append(load)
+    meet(z, devices)
+
+    def span(item, part, source):
+        return pl.ds(pl.multiple_of(source * shard[item] + part * piece[item], 8), piece[item])
+
+    def remote(src, dst, send, recv, name):
+        return pltpu.make_async_remote_copy(
+            src_ref=src, dst_ref=dst, send_sem=send, recv_sem=recv, device_id=devices[name], device_id_type=MESH
+        )
+
+    def c_copy(item, part, side, source):
+        return remote(
+            ins[item][2 * side + 1].at[span(item, part, source)],
+            held[item][1].at[side, span(item, part, source)],
+            side_sem.at[2 + side, item],
+            c_sem.at[item, part, side, source],
+            "c",
+        )
+
+    def x_copy(item, part, source):
+        place = source if part == 0 else source // 2
+        return remote(
+            held[item][0].at[1, span(item, part, source)],
+            held[item][2 + part].at[place],
+            side_sem.at[0, item],
+            x_sem.at[item, part, place],
+            "x",
+        )
+
+    def y_copy(item, part, side, source):
+        return remote(
+            held[item][0].at[side, span(item, part, source)],
+            held[item][4].at[source // 2] if part == 0 else held[item][5].at[side, source // 2],
+            side_sem.at[1, item],
+            y_sem.at[item, part + side, source // 2],
+            "y",
+        )
+
+    def z_copy(item, part, source, away, upward):
+        return remote(
+            held[item][0].at[0, span(item, part, source)],
+            held[item][6].at[1 - upward, part, away],
+            zs_sem.at[item, part, 1 - upward, away],
+            zr_sem.at[item, part, 1 - upward, away],
+            "up" if upward else "down",
+        )
+
+    def add(item, side, part, source, *others):
+        total = held[item][0]
+        start = source * shard[item] + part * piece[item]
+        step = 16
+
+        def one(turn, _):
+            here = pl.ds(pl.multiple_of(start + turn * step, 8), step)
+            value = total[side, here].astype(jnp.float32)
+            for other in others:
+                value = value + other(turn * step, step)
+            total[side, here] = value.astype(jnp.bfloat16)
+            return 0
+
+        lax.fori_loop(0, piece[item] // step, one, 0)
+
+    def c_part(item, side, part, source):
+        start = source * shard[item] + part * piece[item]
+        return lambda at, step: held[item][1][side, pl.ds(pl.multiple_of(start + at, 8), step)].astype(jnp.float32)
+
+    def of(ref, *place):
+        return lambda at, step: ref[(*place, pl.ds(pl.multiple_of(at, 8), step))].astype(jnp.float32)
+
+    def targets(action):
+        def one(turn, _):
+            away = 3 - turn // 2
+            pl.when((turn % 2 == 0) & (z + away <= 3))(lambda: action(column + 2 * away, away, 1))
+            pl.when((turn % 2 == 1) & (z >= away))(lambda: action(column - 2 * away, away, 0))
+            return 0
+
+        lax.fori_loop(0, 6, one, 0)
+        action(column, 0, None)
+
+    def mirror(source):
+        return source + 1 - 2 * (source % 2)
+
+    def send_c(item):
+        def action(source, away, upward):
+            c_copy(item, 0, 1, source).start()
+            c_copy(item, 0, 1, mirror(source)).start()
+            c_copy(item, 1, 1, mirror(source)).start()
+            c_copy(item, 1, 0, mirror(source)).start()
+            c_copy(item, 0, 0, source).start()
+            c_copy(item, 0, 0, mirror(source)).start()
+            c_copy(item, 1, 1, source).start()
+            c_copy(item, 1, 0, source).start()
+
+        targets(action)
+
+    def first(item):
+        def action(source, away, upward):
+            for place in (source, mirror(source)):
+                c_copy(item, 0, 1, place).wait_recv()
+                add(item, 1, 0, place, c_part(item, 1, 0, place))
+                x_copy(item, 0, place).start()
+            for side in (1, 0):
+                place = mirror(source)
+                c_copy(item, 1, side, place).wait_recv()
+                add(item, side, 1, place, c_part(item, side, 1, place))
+                y_copy(item, 1, side, place).start()
+
+        targets(action)
+
+    def second(item):
+        def action(source, away, upward):
+            place = mirror(source)
+            c_copy(item, 0, 0, place).wait_recv()
+            x_copy(item, 0, place).wait_recv()
+            add(item, 0, 0, place, c_part(item, 0, 0, place), of(held[item][2], place))
+            y_copy(item, 0, 0, place).start()
+            c_copy(item, 1, 1, source).wait_recv()
+            y_copy(item, 1, 1, source).wait_recv()
+            add(item, 1, 1, source, c_part(item, 1, 1, source), of(held[item][5], 1, source // 2))
+            x_copy(item, 1, source).start()
+
+        targets(action)
+
+    def third(item):
+        def action(source, away, upward):
+            for part in range(2):
+                c_copy(item, part, 0, source).wait_recv()
+                x_copy(item, part, source).wait_recv()
+                y_copy(item, part, 0, source).wait_recv()
+                if part == 0:
+                    terms = [of(held[item][2], source), of(held[item][4], source // 2)]
+                else:
+                    terms = [of(held[item][3], source // 2), of(held[item][5], 0, source // 2)]
+                add(item, 0, part, source, c_part(item, 0, part, source), *terms)
+                if upward is None:
+                    continue
+                behind = z > 0 if upward else z < 3
+
+                def more():
+                    z_copy(item, part, source, away, upward).wait_recv()
+                    add(item, 0, part, source, of(held[item][6], 1 - upward, part, away))
+
+                pl.when(behind)(more)
+                z_copy(item, part, source, away - 1, upward).start()
+
+        targets(action)
+
+    def last(item):
+        for part in range(2):
+            for upward in (1, 0):
+                pl.when(z > 0 if upward else z < 3)(
+                    lambda: z_copy(item, part, column, 0, upward).wait_recv()
+                )
+            start = column * shard[item] + part * piece[item]
+
+            def one(turn, _):
+                at = pl.multiple_of(turn * 16, 8)
+                value = held[item][0][0, pl.ds(pl.multiple_of(start + at, 8), 16)].astype(jnp.float32)
+                below = held[item][6][0, part, 0, pl.ds(at, 16)].astype(jnp.float32)
+                above = held[item][6][1, part, 0, pl.ds(at, 16)].astype(jnp.float32)
+                value = value + jnp.where(z > 0, below, 0.0) + jnp.where(z < 3, above, 0.0)
+                outs[item][pl.ds(pl.multiple_of(part * piece[item] + at, 8), 16)] = value
+                return 0
+
+            lax.fori_loop(0, piece[item] // 16, one, 0)
+
+    for item in range(items):
+        send_c(item)
+    for load in loads:
+        load.wait()
+    for action in (first, second, third, last):
+        for item in range(items):
+            action(item)
+    for item in range(items):
+        for way, count in enumerate((12, 12, 16, 16)):
+            lead = held[item][0].at[0, pl.ds(0, count * piece[item])]
+            remote(lead, lead, side_sem.at[way, item], load_sem.at[item, 0], "x").wait_send()
+        for part in range(2):
+            for away in range(3):
+                pl.when((z < 3) & (z + away + 1 <= 3))(
+                    lambda: z_copy(item, part, column, away, 1).wait_send()
+                )
+                pl.when((z > 0) & (z - away - 1 >= 0))(
+                    lambda: z_copy(item, part, column, away, 0).wait_send()
+                )
+
+
+def reduce_kernel(grads, tag):
+    items = len(grads)
+    anywhere = pl.BlockSpec(memory_space=pl.ANY)
+    inside = pl.BlockSpec(memory_space=pltpu.VMEM)
+    whole = lax.axis_size("dp")
+    shapes, scratch = [], []
+    for quarters in grads:
+        rows, width = quarters[0].shape
+        half = rows // (2 * whole)
+        shapes.append(jax.ShapeDtypeStruct((rows // whole, width), jnp.float32))
+        for lead in ((2, rows), (2, rows), (8, half), (4, half), (4, half), (2, 4, half), (2, 2, 3, half)):
+            scratch.append(pltpu.VMEM((*lead, width), jnp.bfloat16))
+    return pl.pallas_call(
+        functools.partial(reduce_body, items),
+        name="reduce_grads",
+        out_shape=shapes,
+        in_specs=[anywhere] * (4 * items),
+        out_specs=[inside] * items,
+        scratch_shapes=scratch
+        + [
+            pltpu.SemaphoreType.DMA((items, 2)),
+            pltpu.SemaphoreType.DMA((4, items)),
+            pltpu.SemaphoreType.DMA((items, 2, 2, 8)),
+            pltpu.SemaphoreType.DMA((items, 2, 8)),
+            pltpu.SemaphoreType.DMA((items, 3, 4)),
+            pltpu.SemaphoreType.DMA((items, 2, 2, 3)),
+            pltpu.SemaphoreType.DMA((items, 2, 2, 3)),
+        ],
+        compiler_params=pltpu.CompilerParams(
+            collective_id=tag, has_side_effects=True, vmem_limit_bytes=60 << 20
+        ),
+    )(*[item for quarters in grads for item in quarters])
+
+
+def known_mesh():
+    return lax.axis_size("dp") == 8 and lax.axis_size("tensor") == 4
+
+
+def gather_weights(shards):
+    if not known_mesh():
+        return [gather_all(item, True) for item in shards]
+    return [[item[0], item[2], item[1], item[3]] for item in gather_kernel(shards)]
+
+
+def reduce_grads(grads, tag):
+    if not known_mesh():
+        return [reduce_all(item, True) for item in grads]
+    return reduce_kernel([[item[0], item[2], item[1], item[3]] for item in grads], tag)
 
 
 def wide(value):
@@ -213,20 +660,16 @@
     rows = tokens.shape[0] // parts
     vocab_part, head_part = table.shape[0], joint_weight.shape[1]
     out_part, ff_part = output_weight.shape[0], upward_weight.shape[1]
-    half_vocab = vocab_part // 2
-
-    table_t = narrow(table).T
-    left_half = gather_all(table_t[:, :half_vocab], True)
-    right_half = gather_all(table_t[:, half_vocab:], False)
+
     gain_columns = jnp.pad(narrow(gains).T, ((0, 0), (0, 61)))
-    first_group = gather_all(jnp.concatenate([narrow(joint_weight), gain_columns], axis=1), True)
-    second_group = gather_all(
+    shards = [
+        narrow(table).T,
+        jnp.concatenate([narrow(joint_weight), gain_columns], axis=1),
         jnp.concatenate(
             [narrow(upward_weight), narrow(downward_weight).T, narrow(output_weight).T], axis=1
         ),
-        True,
-    )
-    table_q = [piece for pair in zip(left_half, right_half) for piece in pair]
+    ]
+    table_q, first_group, second_group = gather_weights(shards)
     joint_q = [item[:, :head_part] for item in first_group]
     gain_full = wide(first_group[0][:, head_part : head_part + 3]).T
     up_q = [item[:, :ff_part] for item in second_group]
@@ -260,10 +703,8 @@
     same_doc = segment[:, None] == segment[None, :]
 
     def hot(ids, piece):
-        quarter, side = piece // 2, piece % 2
-        owner = place ^ (2 * (quarter % 2) + quarter // 2)
-        base = owner * vocab_part + side * half_vocab
-        return (ids - base)[:, None] == jnp.arange(half_vocab, dtype=jnp.int32)[None, :]
+        base = (place ^ (2 * (piece % 2) + piece // 2)) * vocab_part
+        return (ids - base)[:, None] == jnp.arange(vocab_part, dtype=jnp.int32)[None, :]
 
     pieces = range(len(table_q))
     input_hot = [narrow(hot(inputs, piece)) for piece in pieces]
@@ -320,20 +761,16 @@
     mlp_grad, gain_three = norm_back(after_mlp, gain_full[2], out_grad)
     mlp_branch = narrow(mlp_grad)
     down_grad = [narrow(mm_tn(mlp_branch, item)) for item in activated]
-    down_sum = reduce_all(down_grad, True)
     up_input = [
         narrow(gelu_pairs[q][1](mm(mlp_branch, down_q[q]))[0]) for q in range(4)
     ]
     up_grad = [narrow(mm_tn(normed_two, item)) for item in up_input]
-    up_sum = reduce_all(up_grad, False)
     normed_two_grad = sum(mm_nt(up_input[q], up_q[q]) for q in range(4))
     attn_in_grad, gain_two = norm_back(after_attn, gain_full[1], normed_two_grad)
     resid_one = mlp_grad + attn_in_grad
     attn_branch = narrow(resid_one)
     out_grads = narrow(mm_tn(attn_branch, attended_all))
-    out_sum = reduce_all(
-        [out_grads[:, q * out_part : (q + 1) * out_part] for q in range(4)], False
-    )
+    out_grad_q = [out_grads[:, q * out_part : (q + 1) * out_part] for q in range(4)]
     attended_grad = narrow(mm(attn_branch, out_all))
     grad_parts = [attended_grad[:, q * out_part : (q + 1) * out_part] for q in range(4)]
     proj_whole = [
@@ -359,17 +796,17 @@
     joint_grad = [
         jnp.concatenate([narrow(mm_tn(normed_one, item)), gain_grad], axis=1) for item in proj_grad
     ]
-    joint_sum = reduce_all(joint_grad, True)
     embed_scaled = narrow(embed_grad * D**0.5)
     table_grad = [
         narrow(mm_tn(normed_out, logit_grad[piece]) + mm_tn(embed_scaled, input_hot[piece]))
         for piece in pieces
     ]
-    table_left = reduce_all(table_grad[0::2], True)
-    table_right = reduce_all(table_grad[1::2], False)
+    table_sum, joint_sum, up_sum, down_sum, out_sum = reduce_grads(
+        [table_grad, joint_grad, up_grad, down_grad, out_grad_q], 1
+    )
     gain_sum = joint_sum[:, head_part : head_part + 3].T
     reduced = (
-        jnp.concatenate([table_left, table_right], axis=1).T,
+        table_sum.T,
         joint_sum[:, :head_part],
         out_sum.T,
         up_sum,

time: 694 us -> 613 us (0.88)
  Pallas kernels: 0 us -> 274 us
  waiting for transfers between devices: 219 us -> 8.04 us
  starting transfers between devices: 93.5 us -> 9.05 us
  matrix products: 205 us -> 168 us
  local copies, waits for them, and re-layouts: 78.8 us -> 51.3 us
    pallas_call x0 -> x2, Pallas kernels: none -> 274 us  [the longest x1 154 us: reduce_kernel(): pl.pallas_call(functools.partial(reduce_body, items), name='reduce_grads'...]
    ppermute x88 -> x14, waiting for transfers between devices: 219 us -> 8.04 us  [swap(): lax.ppermute(value, axis, [(place, place ^ mask) for place in range(size)])]
    ppermute x88 -> x14, starting transfers between devices: 93.5 us -> 9.05 us  [swap(): lax.ppermute(value, axis, [(place, place ^ mask) for place in range(size)])]
    dot_general x29 -> x21, matrix products: 57.5 us -> 38.2 us  [mm_nt(): lax.dot_general(left, right, (((1,), (1,)), ((), ())), preferred_element_...]
    unnamed x418 -> x320, local copies, waits for them, and re-layouts: 41.4 us -> 23.4 us
    dot_general x21 -> x17, matrix products: 55.6 us -> 37.9 us  [mm(): return jnp.dot(left, right, preferred_element_type=jnp.float32)]
    concatenate x7 -> x0, local copies, waits for them, and re-layouts: 14.5 us -> none  [the longest x6 13.6 us: spread(): jnp.concatenate([value] + [swap(value, 'dp', mask) for mask in masks], ax...]
    convert_element_type x0 -> x5, local copies, waits for them, and re-layouts: none -> 7.38 us  [narrow(): return value.astype(jnp.bfloat16)]
  transfers between devices with their start and end apart: 88 -> 14, of which waited for: 32 -> 6; matrix products, arithmetic and copies ran while one was open for 30% -> 13% of each run, Pallas kernels for 0% -> 0%
where the time goes in v2:
time: 613 us; the launch traced here: 602 us
  Pallas kernels  274 us (45%)
  matrix products  168 us (27%)
  other arithmetic  77.1 us (13%)
  local copies, waits for them, and re-layouts  51.3 us (8%)
  between operations  14.9 us (2%)
  starting transfers between devices  9.05 us (1%)
  waiting for transfers between devices  8.04 us (1%)
    pallas_call x1, Pallas kernels, reduce_kernel(): pl.pallas_call(functools.partial(reduce_body, items), name='reduce_grads'...  154 us
    pallas_call x1, Pallas kernels, gather_kernel(): pl.pallas_call(functools.partial(gather_body, items), name='gather_weight...  120 us
    dot_general x21, matrix products, mm_tn(): lax.dot_general(left, right, (((0,), (0,)), ((), ())), preferred_element_...  45.8 us
    dot_general x21, matrix products, mm_nt(): lax.dot_general(left, right, (((1,), (1,)), ((), ())), preferred_element_...  38.2 us
    dot_general x17, matrix products, mm(): return jnp.dot(left, right, preferred_element_type=jnp.float32)  37.9 us
    unnamed x320, local copies, waits for them, and re-layouts  23.4 us
    dot_general x2, matrix products, attend_back(): jnp.einsum('qhe,khe->hqk', grad_out, value_rows, preferred_element_type=j...  12.4 us
  transfers between devices with their start and end apart: 14, of which 6 were waited for; matrix products, arithmetic and copies ran while one was open for 13% of the time, Pallas kernels for 0%

profile of v2, /device:TPU:0, one launch (start us, length us, event | category | flops | bytes accessed | tf_op | source)
XLA Modules:
  0.0 602.0 jit_solution(16212020714019953638)
XLA Ops:
  8.5 119.7 %gather_weights.1 = (bf16[768,2048]{1,0:T(8,128)(2,1)}, bf16[768,2048]{1,0:T(8,128)(2,1)}, bf16[768,2048]{1,0:T(8,128)(2,1)}, bf16[768,2048]{1,0:T(8,128)(2,1)},...) custom-call(bf16[96,2048]{1,0:T(8,128)(2,1)} %convert_bitcast_fusion, ...), custom_call_target="tpu_custom_call" | custom-call | tf_op jit(solution)/shard_map/gather_weights/pallas_call | solution.py:255
  133.1 4.0 fusion.13
  168.5 2.7 fusion.180
  173.0 2.9 copy-done.1
  175.8 2.7 fusion.72
  180.0 2.7 fusion.181
  184.4 2.8 copy-done
  193.1 5.4 multiply_convert_fusion.8
  198.5 5.6 multiply_convert_fusion.9
  204.1 5.4 multiply_convert_fusion.11
  209.6 5.6 multiply_convert_fusion.10
  227.6 5.0 select_reduce_fusion.2
  233.2 8.1 %multiply_convert_fusion.2 = (bf16[512,2048]{1,0:T(8,128)(2,1)S(1)}, bf16[512,2048]{1,0:T(8,128)(2,1)}, bf16[512,2048]{1,0:T(8,128)(2,1)S(1)}, bf16[512,2048]{1,0:T(8,128)(2,1)}) fusion(f32[512,2048]{1,0:T(8,128)S(1)} %get-tuple-element.317, s32[512]{0:T(512)S(1)} %copy-done.96, f32[512]{0:T(512)S(1)} %get-tuple-element.193, f32[512]{0:T(512)S(1)} %copy-done.101, ...), kind=kLoop, calls=%fused_computation.30 | loop fusion | flops 25165824 | bytes 25178112 | tf_op jit(solution)/shard_map/convert_element_type | solution.py:533
  241.3 5.9 fusion.188
  287.1 7.2 %fusion.65 = bf16[1024,3,1,64]{0,3,1,2:T(8,128)(2,1)S(1)} fusion(bf16[1024,3,64]{0,2,1:T(8,128)(2,1)S(1)} %bitcast.300, f32[3,1024,1024]{1,2,0:T(8,128)} %copy-done.1, f32[3,1024]{1,0:T(4,128)S(1)} %log_add_fusion), kind=kOutput, calls=%fused_computation.180 | convolution fusion | flops 409141248 | bytes 13381632 | tf_op jit(solution)/shard_map/hqk,qhe->khe/dot_general | solution.py:616
  294.3 6.2 %multiply_reduce_fusion = (f32[3,1024]{1,0:T(4,128)S(1)}, f32[3,1024,1024]{1,2,0:T(8,128)S(1)}) fusion(f32[3,1024,1024]{1,2,0:T(8,128)} %copy-done.1, f32[3,1024]{1,0:T(4,128)S(1)} %log_add_fusion, bf16[1024,3,64]{0,2,1:T(8,128)(2,1)S(1)} %bitcast.301, bf16[1024,3,3,64]{0,3,2,1:T(8,128)(2,1)S(1)} %bitcast.290), kind=kOutput, calls=%fused_computation.1 | convolution fusion | flops 412087296 | bytes 25980928 | tf_op jit(solution)/shard_map/qhe,khe->hqk/dot_general | solution.py:619
  301.3 5.2 multiply_convert_fusion
  306.6 5.0 fusion.54
  311.6 2.9 fusion.53
  317.7 6.2 %multiply_reduce_fusion.1 = (f32[3,1024]{1,0:T(4,128)S(1)}, f32[3,1024,1024]{1,2,0:T(8,128)S(1)}) fusion(f32[3,1024,1024]{1,2,0:T(8,128)} %copy-done, f32[3,1024]{1,0:T(4,128)S(1)} %copy-done.49, bf16[1024,3,64]{0,2,1:T(8,128)(2,1)S(1)} %bitcast.298, bf16[1024,3,3,64]{0,3,2,1:T(8,128)(2,1)S(1)} %bitcast.295), kind=kOutput, calls=%fused_computation.4 | convolution fusion | flops 412087296 | bytes 25980928 | tf_op jit(solution)/shard_map/qhe,khe->hqk/dot_general | solution.py:619
  326.0 5.2 multiply_convert_fusion.1
  331.2 5.0 fusion.55
  346.0 2.7 convolution_convert_fusion.10
  367.8 3.7 add_convert_fusion.3.refs_0_
  371.5 3.5 add_convert_fusion.2.refs_1_
  375.1 3.6 add_convert_fusion.1.refs_2_
  378.7 3.6 add_convert_fusion.refs_3_
  385.6 2.8 convolution_convert_fusion.11
  390.5 3.7 fusion.114
  394.3 154.0 %reduce_grads.1 = (f32[96,2048]{1,0:T(8,128)}, f32[96,640]{1,0:T(8,128)}, f32[96,768]{1,0:T(8,128)}, f32[96,768]{1,0:T(8,128)}, f32[96,192]{1,0:T(8,128)}) custom-call(bf16[768,2048]{1,0:T(8,128)(2,1)} %add_convert_fusion.3.refs_0_, bf16[768,2048]{1,0:T(8,128)(2,1)} %add_convert_fusion.2.refs_1_, bf16[768,2048]{1,0:T(8,128)(2,1)} %add_convert_fusion.1.refs_2_, ...), custom_call_target="tpu_custom_call" | custom-call | tf_op jit(solution)/shard_map/reduce_grads/pallas_call | solution.py:490
  569.4 2.6 collective-permute-start.9
  590.8 3.5 multiply_subtract_fusion
  (526 shorter events, 181.9 us)
Async XLA Ops:
  4.6 124.6 %copy-start.45 = (f32[192,96]{0,1:T(8,128)}, f32[192,96]{0,1:T(8,128)S(1)}, u32[]{:S(2)}) copy-start(f32[192,96]{0,1:T(8,128)S(1)} %copy.282) | copy-start | bytes 221188
  5.1 125.3 %copy-start.104 = (pred[1024]{0:T(1024)(128)(4,1)}, pred[1024]{0:T(1024)(128)(4,1)S(1)}, u32[]{:S(2)}) copy-start(pred[1024]{0:T(1024)(128)(4,1)S(1)} %broadcast_compare_fusion.1) | copy-start | bytes 3076
  130.3 13.9 %copy-start.80 = (f32[768]{0:T(1024)}, f32[768]{0:T(1024)S(1)}, u32[]{:S(2)}) copy-start(f32[768]{0:T(1024)S(1)} %get-tuple-element.170) | copy-start | bytes 9220
  143.6 47.6 %copy-start.6 = (f32[512,768]{1,0:T(8,128)}, f32[512,768]{1,0:T(8,128)S(1)}, u32[]{:S(2)}) copy-start(f32[512,768]{1,0:T(8,128)S(1)} %get-tuple-element.303) | copy-start | bytes 4718596
  150.5 16.8 %collective-permute-start.1 = (bf16[512,576]{0,1:T(8,128)(2,1)}, bf16[512,576]{0,1:T(8,128)(2,1)}, u32[]{:S(2)}, u32[]{:S(2)}) collective-permute-start(bf16[512,576]{0,1:T(8,128)(2,1)} %bitcast.40), channel_id=1, source_target_pairs={{0,1},{1,0},{2,3},{3,2},{4,5},{5,4},{6,7},{7,6},{8,9},{9,8},{10,11... | collective-permute-start | bytes 1769480 | tf_op jit(solution)/shard_map/ppermute | solution.py:64
  153.9 24.9 %collective-permute-start = (bf16[512,576]{0,1:T(8,128)(2,1)}, bf16[512,576]{0,1:T(8,128)(2,1)}, u32[]{:S(2)}, u32[]{:S(2)}) collective-permute-start(bf16[512,576]{0,1:T(8,128)(2,1)} %bitcast.22), channel_id=1, source_target_pairs={{0,1},{1,0},{2,3},{3,2},{4,5},{5,4},{6,7},{7,6},{8,9},{9,8},{10,11... | collective-permute-start | bytes 1769480 | tf_op jit(solution)/shard_map/ppermute | solution.py:64
  178.6 12.6 %copy-start.73 = (bf16[512,3,64]{0,2,1:T(8,128)(2,1)}, bf16[512,3,64]{0,2,1:T(8,128)(2,1)S(1)}, u32[]{:S(2)}) copy-start(bf16[512,3,64]{0,2,1:T(8,128)(2,1)S(1)} %get-tuple-element.248) | copy-start | bytes 589828
  178.6 12.1 %collective-permute-start.3 = (bf16[512,192]{0,1:T(8,128)(2,1)S(1)}, bf16[512,192]{0,1:T(8,128)(2,1)S(1)}, u32[]{:S(2)}, u32[]{:S(2)}) collective-permute-start(bf16[512,192]{0,1:T(8,128)(2,1)S(1)} %bitcast.327), channel_id=1, source_target_pairs={{0,1},{1,0},{2,3},{3,2},{4,5},{5,4},{6,7},{7,6},{8,9},{9,8},{10,11... | collective-permute-start | bytes 589832 | tf_op jit(solution)/shard_map/ppermute | solution.py:64
  189.6 1.6 collective-permute-start.2
  198.5 19.2 %copy-start.53 = (bf16[512,768]{1,0:T(8,128)(2,1)}, bf16[512,768]{1,0:T(8,128)(2,1)S(1)}, u32[]{:S(2)}) copy-start(bf16[512,768]{1,0:T(8,128)(2,1)S(1)} %get-tuple-element.194) | copy-start | bytes 2359300
  204.1 11.1 %copy-start.132 = (bf16[512,768]{1,0:T(8,128)(2,1)}, bf16[512,768]{1,0:T(8,128)(2,1)S(1)}, u32[]{:S(2)}) copy-start(bf16[512,768]{1,0:T(8,128)(2,1)S(1)} %get-tuple-element.200) | copy-start | bytes 2359300
  282.7 4.1 collective-permute-start.5
  283.1 31.4 %collective-permute-start.4 = (bf16[512,192]{1,0:T(8,128)(2,1)}, bf16[512,192]{1,0:T(8,128)(2,1)}, u32[]{:S(2)}, u32[]{:S(2)}) collective-permute-start(bf16[512,192]{1,0:T(8,128)(2,1)} %get-tuple-element.228), channel_id=1, source_target_pairs={{0,1},{1,0},{2,3},{3,2},{4,5},{5,4},{6,7},{7,6},{8,9},{9,8},{10,11... | collective-permute-start | bytes 589832 | tf_op jit(solution)/shard_map/ppermute | solution.py:64
  287.1 13.4 %slice-start.3 = ((s8[12582912]{0:T(1024)(128)(4,1)}), s8[4194304]{0:T(1024)(128)(4,1)S(1)}, s32[]{:S(2)}) async-start(s8[12582912]{0:T(1024)(128)(4,1)} %bitcast.286), calls=%async_computation.3 | async-start | bytes 8388608
  341.3 15.2 %collective-permute-start.7 = (bf16[512,576]{0,1:T(8,128)(2,1)}, bf16[512,576]{0,1:T(8,128)(2,1)}, u32[]{:S(2)}, u32[]{:S(2)}) collective-permute-start(bf16[512,576]{0,1:T(8,128)(2,1)} %bitcast.67), channel_id=1, source_target_pairs={{0,1},{1,0},{2,3},{3,2},{4,5},{5,4},{6,7},{7,6},{8,9},{9,8},{10,11... | collective-permute-start | bytes 1769480 | tf_op jit(solution)/shard_map/ppermute | solution.py:64
  342.8 11.2 %collective-permute-start.6 = (bf16[512,576]{0,1:T(8,128)(2,1)}, bf16[512,576]{0,1:T(8,128)(2,1)}, u32[]{:S(2)}, u32[]{:S(2)}) collective-permute-start(bf16[512,576]{0,1:T(8,128)(2,1)} %bitcast.66), channel_id=1, source_target_pairs={{0,1},{1,0},{2,3},{3,2},{4,5},{5,4},{6,7},{7,6},{8,9},{9,8},{10,11... | collective-permute-start | bytes 1769480 | tf_op jit(solution)/shard_map/ppermute | solution.py:64
  548.3 33.6 %copy-start.46 = (f32[192,96]{0,1:T(8,128)S(1)}, f32[192,96]{0,1:T(8,128)}, u32[]{:S(2)}) copy-start(f32[192,96]{0,1:T(8,128)} %copy-done.45) | copy-start | bytes 221188
  548.3 33.6 %copy-start.63 = (f32[192,96]{0,1:T(8,128)S(1)}, f32[192,96]{0,1:T(8,128)}, u32[]{:S(2)}) copy-start(f32[192,96]{0,1:T(8,128)} %copy.325) | copy-start | bytes 221188
  548.3 33.6 %copy-start.64 = (f32[192,96]{0,1:T(8,128)S(1)}, f32[192,96]{0,1:T(8,128)}, u32[]{:S(2)}) copy-start(f32[192,96]{0,1:T(8,128)} %copy.324) | copy-start | bytes 221188
  548.3 33.6 %copy-start.65 = (f32[96,192]{1,0:T(8,128)S(1)}, f32[96,192]{1,0:T(8,128)}, u32[]{:S(2)}) copy-start(f32[96,192]{1,0:T(8,128)} %get-tuple-element.51) | copy-start | bytes 221188
  548.4 38.0 %copy-start.36 = (f32[96,640]{1,0:T(8,128)S(1)}, f32[96,640]{1,0:T(8,128)}, u32[]{:S(2)}) copy-start(f32[96,640]{1,0:T(8,128)} %get-tuple-element.50) | copy-start | bytes 737284
  548.4 38.0 %copy-start.72 = (f32[3,96]{0,1:T(8,128)S(1)}, f32[3,96]{0,1:T(8,128)}, u32[]{:S(2)}) copy-start(f32[3,96]{0,1:T(8,128)} %copy.330) | copy-start | bytes 3460
  551.5 37.7 %copy-start.98 = (f32[3,96]{1,0:T(4,128)S(1)}, f32[3,96]{1,0:T(4,128)}, u32[]{:S(2)}) copy-start(f32[3,96]{1,0:T(4,128)} %param.33) | copy-start | bytes 3460
  553.5 37.3 %copy-start.24 = (f32[2048,96]{0,1:T(8,128)S(1)}, f32[2048,96]{0,1:T(8,128)}, u32[]{:S(2)}) copy-start(f32[2048,96]{0,1:T(8,128)} %param.28) | copy-start | bytes 2359300
  553.5 37.3 %copy-start.25 = (f32[96,2048]{1,0:T(8,128)S(1)}, f32[96,2048]{1,0:T(8,128)}, u32[]{:S(2)}) copy-start(f32[96,2048]{1,0:T(8,128)} %get-tuple-element.49) | copy-start | bytes 2359300
  553.5 37.3 %copy-start.50 = (f32[2048,96]{0,1:T(8,128)S(1)}, f32[2048,96]{0,1:T(8,128)}, u32[]{:S(2)}) copy-start(f32[2048,96]{0,1:T(8,128)} %param.40) | copy-start | bytes 2359300
  562.8 3.5 collective-permute-start.8
  567.7 5.3 collective-permute-start.11
  568.5 4.5 collective-permute-start.10
  569.4 4.1 collective-permute-start.9
  573.6 1.1 collective-permute-start.12
  574.7 3.5 collective-permute-start.13
  (134 other events, 441.7 us)

commit v3 on v2

--- a/solution.py
+++ b/solution.py
@@ -269,26 +269,40 @@
     return [flat[4 * item : 4 * item + 4] for item in range(items)]
 
 
-def reduce_body(items, *refs):
-    ins = [refs[4 * item : 4 * item + 4] for item in range(items)]
-    outs = refs[4 * items : 5 * items]
-    held = [refs[5 * items + 7 * item : 5 * items + 7 * item + 7] for item in range(items)]
-    load_sem, side_sem, c_sem, x_sem, y_sem, zs_sem, zr_sem = refs[12 * items :]
+def reduce_body(layout, parts, gains_at, *refs):
+    items, arrays = len(layout), sum([len(item) for item in layout])
+    ins = [refs[4 * array : 4 * array + 4] for array in range(arrays)]
+    facts = refs[4 * arrays]
+    refs = refs[4 * arrays + 1 :]
+    outs, totals = refs[:items], refs[items]
+    refs = refs[items + 1 :]
+    held = [refs[7 * item : 7 * item + 7] for item in range(items)]
+    load_sem, side_sem, c_sem, x_sem, y_sem, zs_sem, zr_sem, whole_send, whole_recv = refs[7 * items : 7 * items + 9]
+    tile, tile_row, tile_column, row_send, row_recv, column_send, column_recv = refs[7 * items + 9 :]
     column = lax.axis_index("dp")
     z, y = column // 2, column % 2
     devices = neighbours()
     shard = [item.shape[0] for item in outs]
     piece = [item // 2 for item in shard]
 
-    loads = []
+    loads = [[] for _ in range(items)]
     for item in range(items):
-        for side in range(2):
-            load = pltpu.make_async_copy(
-                ins[item][2 * side], held[item][0].at[side], load_sem.at[item, side]
-            )
-            load.start()
-            loads.append(load)
-    meet(z, devices)
+        for array, at, width in layout[item]:
+            for side in range(2):
+                load = pltpu.make_async_copy(
+                    ins[array][2 * side],
+                    held[item][0].at[side, :, pl.ds(at, width)],
+                    load_sem.at[array, side],
+                )
+                load.start()
+                loads[item].append(load)
+    row = lax.axis_index("tensor")
+    row_peers = [(column, (row + away) % 4) for away in (1, 2, 3)]
+    column_peers = [((column + away) % 8, row) for away in range(1, 8)]
+    barrier = pltpu.get_barrier_semaphore()
+    for device in row_peers + column_peers:
+        pl.semaphore_signal(barrier, inc=1, device_id=device, device_id_type=MESH)
+    pl.semaphore_wait(barrier, 10)
 
     def span(item, part, source):
         return pl.ds(pl.multiple_of(source * shard[item] + part * piece[item], 8), piece[item])
@@ -299,13 +313,31 @@
         )
 
     def c_copy(item, part, side, source):
+        array = layout[item][0][0]
         return remote(
-            ins[item][2 * side + 1].at[span(item, part, source)],
+            ins[array][2 * side + 1].at[span(item, part, source)],
             held[item][1].at[side, span(item, part, source)],
             side_sem.at[2 + side, item],
-            c_sem.at[item, part, side, source],
+            c_sem.at[part, side, source],
             "c",
         )
+
+    def c_whole(item):
+        return [
+            remote(
+                ins[array][2 * side + 1],
+                held[item][1].at[side, :, pl.ds(at, width)],
+                whole_send.at[array, side],
+                whole_recv.at[array, side],
+                "c",
+            )
+            for array, at, width in layout[item]
+            for side in range(2)
+        ]
+
+    def c_wait(item, part, side, source):
+        if item == 0:
+            c_copy(item, part, side, source).wait_recv()
 
     def x_copy(item, part, source):
         place = source if part == 0 else source // 2
@@ -357,85 +389,81 @@
     def of(ref, *place):
         return lambda at, step: ref[(*place, pl.ds(pl.multiple_of(at, 8), step))].astype(jnp.float32)
 
-    def targets(action):
-        def one(turn, _):
-            away = 3 - turn // 2
-            pl.when((turn % 2 == 0) & (z + away <= 3))(lambda: action(column + 2 * away, away, 1))
-            pl.when((turn % 2 == 1) & (z >= away))(lambda: action(column - 2 * away, away, 0))
-            return 0
-
-        lax.fori_loop(0, 6, one, 0)
-        action(column, 0, None)
-
     def mirror(source):
         return source + 1 - 2 * (source % 2)
 
-    def send_c(item):
-        def action(source, away, upward):
-            c_copy(item, 0, 1, source).start()
-            c_copy(item, 0, 1, mirror(source)).start()
-            c_copy(item, 1, 1, mirror(source)).start()
-            c_copy(item, 1, 0, mirror(source)).start()
-            c_copy(item, 0, 0, source).start()
-            c_copy(item, 0, 0, mirror(source)).start()
-            c_copy(item, 1, 1, source).start()
-            c_copy(item, 1, 0, source).start()
-
-        targets(action)
-
-    def first(item):
-        def action(source, away, upward):
-            for place in (source, mirror(source)):
-                c_copy(item, 0, 1, place).wait_recv()
-                add(item, 1, 0, place, c_part(item, 1, 0, place))
-                x_copy(item, 0, place).start()
-            for side in (1, 0):
-                place = mirror(source)
-                c_copy(item, 1, side, place).wait_recv()
-                add(item, side, 1, place, c_part(item, side, 1, place))
-                y_copy(item, 1, side, place).start()
-
-        targets(action)
-
-    def second(item):
-        def action(source, away, upward):
-            place = mirror(source)
-            c_copy(item, 0, 0, place).wait_recv()
-            x_copy(item, 0, place).wait_recv()
-            add(item, 0, 0, place, c_part(item, 0, 0, place), of(held[item][2], place))
-            y_copy(item, 0, 0, place).start()
-            c_copy(item, 1, 1, source).wait_recv()
-            y_copy(item, 1, 1, source).wait_recv()
-            add(item, 1, 1, source, c_part(item, 1, 1, source), of(held[item][5], 1, source // 2))
-            x_copy(item, 1, source).start()
-
-        targets(action)
-
-    def third(item):
-        def action(source, away, upward):
+    def target(turn):
+        low = 3 - turn if turn < 2 else jnp.where(z % 3 == 0, 3 - turn, turn - 2)
+        return column + 2 * (jnp.where(z < 2, low, 3 - low) - z)
+
+    def send_c(item, turn):
+        source = target(turn)
+        for part, side, place in (
+            (0, 1, source),
+            (1, 1, mirror(source)),
+            (0, 1, mirror(source)),
+            (1, 0, mirror(source)),
+            (0, 0, mirror(source)),
+            (1, 1, source),
+            (0, 0, source),
+            (1, 0, source),
+        ):
+            c_copy(item, part, side, place).start()
+
+    def first(item, turn):
+        source = target(turn)
+        for x_place, y_side in ((source, 1), (mirror(source), 0)):
+            c_wait(item, 0, 1, x_place)
+            add(item, 1, 0, x_place, c_part(item, 1, 0, x_place))
+            x_copy(item, 0, x_place).start()
+            y_place = mirror(source)
+            c_wait(item, 1, y_side, y_place)
+            add(item, y_side, 1, y_place, c_part(item, y_side, 1, y_place))
+            y_copy(item, 1, y_side, y_place).start()
+
+    def second(item, turn):
+        source = target(turn)
+        place = mirror(source)
+        c_wait(item, 0, 0, place)
+        x_copy(item, 0, place).wait_recv()
+        add(item, 0, 0, place, c_part(item, 0, 0, place), of(held[item][2], place))
+        y_copy(item, 0, 0, place).start()
+        c_wait(item, 1, 1, source)
+        y_copy(item, 1, 1, source).wait_recv()
+        add(item, 1, 1, source, c_part(item, 1, 1, source), of(held[item][5], 1, source // 2))
+        x_copy(item, 1, source).start()
+
+    def third(item, turn):
+        source = target(turn)
+        for part in range(2):
+            c_wait(item, part, 0, source)
+            x_copy(item, part, source).wait_recv()
+            y_copy(item, part, 0, source).wait_recv()
+            if part == 0:
+                terms = [of(held[item][2], source), of(held[item][4], source // 2)]
+            else:
+                terms = [of(held[item][3], source // 2), of(held[item][5], 0, source // 2)]
+            add(item, 0, part, source, c_part(item, 0, part, source), *terms)
+
+    def fourth(item, turn):
+        source = target(turn)
+        away = jnp.where(source > column, source - column, column - source) // 2
+
+        def along(upward):
             for part in range(2):
-                c_copy(item, part, 0, source).wait_recv()
-                x_copy(item, part, source).wait_recv()
-                y_copy(item, part, 0, source).wait_recv()
-                if part == 0:
-                    terms = [of(held[item][2], source), of(held[item][4], source // 2)]
-                else:
-                    terms = [of(held[item][3], source // 2), of(held[item][5], 0, source // 2)]
-                add(item, 0, part, source, c_part(item, 0, part, source), *terms)
-                if upward is None:
-                    continue
-                behind = z > 0 if upward else z < 3
 
                 def more():
                     z_copy(item, part, source, away, upward).wait_recv()
                     add(item, 0, part, source, of(held[item][6], 1 - upward, part, away))
 
-                pl.when(behind)(more)
+                pl.when(z > 0 if upward else z < 3)(more)
                 z_copy(item, part, source, away - 1, upward).start()
 
-        targets(action)
+        pl.when(source > column)(lambda: along(1))
+        pl.when(source < column)(lambda: along(0))
 
     def last(item):
+        square = jnp.zeros((), jnp.float32)
         for part in range(2):
             for upward in (1, 0):
                 pl.when(z > 0 if upward else z < 3)(
@@ -443,26 +471,92 @@
                 )
             start = column * shard[item] + part * piece[item]
 
-            def one(turn, _):
+            def one(turn, square):
                 at = pl.multiple_of(turn * 16, 8)
                 value = held[item][0][0, pl.ds(pl.multiple_of(start + at, 8), 16)].astype(jnp.float32)
                 below = held[item][6][0, part, 0, pl.ds(at, 16)].astype(jnp.float32)
                 above = held[item][6][1, part, 0, pl.ds(at, 16)].astype(jnp.float32)
                 value = value + jnp.where(z > 0, below, 0.0) + jnp.where(z < 3, above, 0.0)
                 outs[item][pl.ds(pl.multiple_of(part * piece[item] + at, 8), 16)] = value
-                return 0
-
-            lax.fori_loop(0, piece[item] // 16, one, 0)
-
+                square_here = value * value
+                if item == gains_at[0]:
+                    lane = lax.broadcasted_iota(jnp.int32, value.shape, 1)
+                    repeated = (lane >= gains_at[1]) & (lane < gains_at[1] + gains_at[2])
+                    square_here = jnp.where(repeated, square_here / parts, square_here)
+                return square + jnp.sum(square_here)
+
+            square = lax.fori_loop(0, piece[item] // 16, one, square)
+        return square
+
+    steps = [(item, turn) for item in range(items) for turn in range(4)]
+    count = len(steps)
+    for turn in range(3):
+        send_c(*steps[turn])
+    for turn in range(count + 3):
+        if turn == 0:
+            send_c(*steps[3])
+        if turn % 4 == 0 and turn + 4 < count:
+            for crossing in c_whole(turn // 4 + 1):
+                crossing.start()
+        if turn < count:
+            if turn % 4 == 0:
+                for load in loads[turn // 4]:
+                    load.wait()
+                if turn > 0:
+                    for crossing in c_whole(turn // 4):
+                        crossing.wait_recv()
+            first(*steps[turn])
+        if 0 <= turn - 1 < count:
+            second(*steps[turn - 1])
+        if 0 <= turn - 2 < count:
+            third(*steps[turn - 2])
+        if 0 <= turn - 3 < count and (turn - 3) % 4 < 3:
+            fourth(*steps[turn - 3])
+    square = sum([last(item) for item in range(items)])
+    sublane = lax.broadcasted_iota(jnp.int32, (8, 128), 0)
+    tile[...] = jnp.where(sublane == 0, square, facts[...])
+
+    def exchange(value, slots, here, peers, sources, send, recv):
+        slots[here] = value
+
+        def crossing(place, device, source):
+            return pltpu.make_async_remote_copy(
+                src_ref=slots.at[here],
+                dst_ref=slots.at[source],
+                send_sem=send.at[place],
+                recv_sem=recv.at[source],
+                device_id=device,
+                device_id_type=MESH,
+            )
+
+        for place, device in enumerate(peers):
+            crossing(place, device, here).start()
+        for place, device in enumerate(peers):
+            crossing(place, device, sources[place]).wait_recv()
+        total = slots[0]
+        for place in range(1, len(peers) + 1):
+            total = total + slots[place]
+        for place, device in enumerate(peers):
+            crossing(place, device, here).wait_send()
+        return total
+
+    along_row = exchange(
+        tile[...], tile_row, row, row_peers, [(row + away) % 4 for away in (1, 2, 3)], row_send, row_recv
+    )
+    totals[...] = exchange(
+        along_row,
+        tile_column,
+        column,
+        column_peers,
+        [(column + away) % 8 for away in range(1, 8)],
+        column_send,
+        column_recv,
+    )
     for item in range(items):
-        send_c(item)
-    for load in loads:
-        load.wait()
-    for action in (first, second, third, last):
-        for item in range(items):
-            action(item)
-    for item in range(items):
-        for way, count in enumerate((12, 12, 16, 16)):
+        if item > 0:
+            for crossing in c_whole(item):
+                crossing.wait_send()
+        for way, count in enumerate((12, 12, 16, 16) if item == 0 else (12, 12)):
             lead = held[item][0].at[0, pl.ds(0, count * piece[item])]
             remote(lead, lead, side_sem.at[way, item], load_sem.at[item, 0], "x").wait_send()
         for part in range(2):
@@ -475,38 +569,107 @@
                 )
 
 
-def reduce_kernel(grads, tag):
-    items = len(grads)
+def reduce_kernel(layout, grads, facts, parts, gains_at, tag):
+    items, arrays = len(layout), len(grads)
     anywhere = pl.BlockSpec(memory_space=pl.ANY)
     inside = pl.BlockSpec(memory_space=pltpu.VMEM)
     whole = lax.axis_size("dp")
+    rows = grads[0][0].shape[0]
+    half = rows // (2 * whole)
     shapes, scratch = [], []
-    for quarters in grads:
-        rows, width = quarters[0].shape
-        half = rows // (2 * whole)
+    for item in layout:
+        width = sum([part[2] for part in item])
         shapes.append(jax.ShapeDtypeStruct((rows // whole, width), jnp.float32))
         for lead in ((2, rows), (2, rows), (8, half), (4, half), (4, half), (2, 4, half), (2, 2, 3, half)):
             scratch.append(pltpu.VMEM((*lead, width), jnp.bfloat16))
-    return pl.pallas_call(
-        functools.partial(reduce_body, items),
+    shapes.append(jax.ShapeDtypeStruct((8, 128), jnp.float32))
+    found = pl.pallas_call(
+        functools.partial(reduce_body, layout, parts, gains_at),
         name="reduce_grads",
         out_shape=shapes,
-        in_specs=[anywhere] * (4 * items),
-        out_specs=[inside] * items,
+        in_specs=[anywhere] * (4 * arrays) + [inside],
+        out_specs=[inside] * (items + 1),
         scratch_shapes=scratch
         + [
-            pltpu.SemaphoreType.DMA((items, 2)),
+            pltpu.SemaphoreType.DMA((arrays, 2)),
             pltpu.SemaphoreType.DMA((4, items)),
-            pltpu.SemaphoreType.DMA((items, 2, 2, 8)),
+            pltpu.SemaphoreType.DMA((2, 2, 8)),
             pltpu.SemaphoreType.DMA((items, 2, 8)),
             pltpu.SemaphoreType.DMA((items, 3, 4)),
             pltpu.SemaphoreType.DMA((items, 2, 2, 3)),
             pltpu.SemaphoreType.DMA((items, 2, 2, 3)),
+            pltpu.SemaphoreType.DMA((arrays, 2)),
+            pltpu.SemaphoreType.DMA((arrays, 2)),
+            pltpu.VMEM((8, 128), jnp.float32),
+            pltpu.VMEM((4, 8, 128), jnp.float32),
+            pltpu.VMEM((8, 8, 128), jnp.float32),
+            pltpu.SemaphoreType.DMA((3,)),
+            pltpu.SemaphoreType.DMA((4,)),
+            pltpu.SemaphoreType.DMA((7,)),
+            pltpu.SemaphoreType.DMA((8,)),
         ],
         compiler_params=pltpu.CompilerParams(
             collective_id=tag, has_side_effects=True, vmem_limit_bytes=60 << 20
         ),
-    )(*[item for quarters in grads for item in quarters])
+    )(*[item for quarters in grads for item in quarters], facts)
+    return found[:-1], found[-1]
+
+
+def update_body(sources, plans, *refs):
+    count = len(plans)
+    totals, fixes, grads = refs[0], refs[1], refs[2 : 2 + sources]
+    refs = refs[2 + sources :]
+    triples = [refs[3 * place : 3 * place + 3] for place in range(count)]
+    outs = [refs[3 * (count + place) : 3 * (count + place) + 3] for place in range(count)]
+    square, loss, real = totals[0:1, :], totals[1:2, :], totals[2:3, :]
+    norm = jnp.sqrt(square) / real
+    refs[6 * count][...] = jnp.concatenate([loss / real, norm] + [norm] * 6, axis=0)
+    scale = (jnp.minimum(1.0, clip_at / norm) / real)[:, 0:1]
+    over_one, over_two = fixes[0:1, 0:1], fixes[1:2, 0:1]
+
+    def renew(place, grad, rows):
+        source, turned, first, rate, decay = plans[place]
+        weight, one, two = triples[place]
+        clipped = grad * scale
+        moment_one = beta_one * one[rows] + (1.0 - beta_one) * clipped
+        moment_two = beta_two * two[rows] + (1.0 - beta_two) * clipped * clipped
+        stepped = moment_one * over_one / (jnp.sqrt(moment_two * over_two) + adam_eps)
+        outs[place][0][rows] = moment_one
+        outs[place][1][rows] = moment_two
+        outs[place][2][rows] = weight[rows] - rate * (stepped + decay * weight[rows])
+
+    for place in range(count):
+        source, turned, first, rate, decay = plans[place]
+        rows, columns = triples[place][0].shape
+        if turned and rows >= 128:
+            for at in range(0, rows, 128):
+                span = min(128, rows - at)
+                block = grads[source][:, first + at : first + at + span].T
+                renew(place, block, pl.ds(at, span))
+        elif turned:
+            start = first // 128 * 128
+            block = grads[source][:, start : start + 128].T
+            renew(place, block[first - start : first - start + rows], pl.ds(0, rows))
+        else:
+            for at in range(0, rows, 32):
+                renew(place, grads[source][pl.ds(at, 32), first : first + columns], pl.ds(at, 32))
+
+
+def update_kernel(totals, fixes, grads, plans, triples):
+    inside = pl.BlockSpec(memory_space=pltpu.VMEM)
+    flat = [item for triple in triples for item in triple]
+    outs = [jax.ShapeDtypeStruct(item.shape, item.dtype) for item in flat] + [
+        jax.ShapeDtypeStruct((8, 128), jnp.float32)
+    ]
+    found = pl.pallas_call(
+        functools.partial(update_body, len(grads), plans),
+        name="update_weights",
+        out_shape=outs,
+        in_specs=[inside] * (2 + len(grads) + len(flat)),
+        out_specs=[inside] * len(outs),
+        compiler_params=pltpu.CompilerParams(vmem_limit_bytes=60 << 20),
+    )(totals, fixes, *grads, *flat)
+    return found[:-1], found[-1]
 
 
 def known_mesh():
@@ -519,10 +682,17 @@
     return [[item[0], item[2], item[1], item[3]] for item in gather_kernel(shards)]
 
 
-def reduce_grads(grads, tag):
-    if not known_mesh():
-        return [reduce_all(item, True) for item in grads]
-    return reduce_kernel([[item[0], item[2], item[1], item[3]] for item in grads], tag)
+def reduce_grads(layout, grads, facts, parts, gains_at):
+    if known_mesh():
+        ordered = [[item[0], item[2], item[1], item[3]] for item in grads]
+        return reduce_kernel(layout, ordered, facts, parts, gains_at, 1)
+    sums = [reduce_all(item, True) for item in grads]
+    sums = [jnp.concatenate([sums[part[0]] for part in item], axis=1) for item in layout]
+    square = sum(jnp.sum(item * item) for item in sums)
+    repeated = sums[gains_at[0]][:, gains_at[1] : gains_at[1] + gains_at[2]]
+    square = square - jnp.sum(repeated * repeated) * (1.0 - 1.0 / parts)
+    tile = jnp.where(lax.broadcasted_iota(jnp.int32, (8, 128), 0) == 0, square, facts)
+    return sums, everyone_sum(tile)
 
 
 def wide(value):
@@ -577,10 +747,6 @@
     return lax.dot_general(left, right, (((0,), (0,)), ((), ())), preferred_element_type=jnp.float32)
 
 
-def gelu_exact(values):
-    return jax.nn.gelu(values, approximate=False)
-
-
 def rotate_heads(values, cosine, sine):
     return rotate(values, cosine[:, None, :], sine[:, None, :])
 
@@ -628,6 +794,24 @@
     query_grad = rotate_heads(query_grad, cosine, -sine)
     key_grad = rotate_heads(key_grad, cosine, -sine)
     return narrow(jnp.stack([query_grad, key_grad, value_grad], axis=2).reshape(packed.shape))
+
+
+def update_weights(totals, fixes, sums, plans, triples):
+    if known_mesh():
+        updated, results = update_kernel(totals, fixes, sums, plans, triples)
+        return list(updated), results
+    updated = []
+    norm = jnp.sqrt(totals[0, 0]) / totals[2, 0]
+    scale = jnp.minimum(1.0, clip_at / norm) / totals[2, 0]
+    for (source, turned, first, rate, decay), (weight, one, two) in zip(plans, triples):
+        columns = weight.shape[0] if turned else weight.shape[1]
+        grad = sums[source][:, first : first + columns]
+        clipped = (grad.T if turned else grad) * scale
+        moment_one = beta_one * one + (1.0 - beta_one) * clipped
+        moment_two = beta_two * two + (1.0 - beta_two) * clipped * clipped
+        stepped = moment_one * fixes[0, 0] / (jnp.sqrt(moment_two * fixes[1, 0]) + adam_eps)
+        updated.extend([moment_one, moment_two, weight - rate * (stepped + decay * weight)])
+    return updated, jnp.stack([totals[1, 0] / totals[2, 0], norm])[:, None]
 
 
 def per_device(
@@ -665,16 +849,14 @@
     shards = [
         narrow(table).T,
         jnp.concatenate([narrow(joint_weight), gain_columns], axis=1),
-        jnp.concatenate(
-            [narrow(upward_weight), narrow(downward_weight).T, narrow(output_weight).T], axis=1
-        ),
-    ]
-    table_q, first_group, second_group = gather_weights(shards)
+        narrow(upward_weight),
+        narrow(downward_weight).T,
+        narrow(output_weight).T,
+    ]
+    table_q, first_group, up_q, down_q, out_q = gather_weights(shards)
     joint_q = [item[:, :head_part] for item in first_group]
     gain_full = wide(first_group[0][:, head_part : head_part + 3]).T
-    up_q = [item[:, :ff_part] for item in second_group]
-    down_q = [item[:, ff_part : 2 * ff_part] for item in second_group]
-    out_all = jnp.concatenate([item[:, 2 * ff_part :] for item in second_group], axis=1)
+    out_all = jnp.concatenate(out_q, axis=1)
 
     start = place * rows
     seq = start // SEQ_LEN
@@ -733,8 +915,12 @@
     after_attn = embedded + mm_nt(attended_all, out_all)
     normed_two = narrow(norm_apply(after_attn, gain_full[1]))
     pre_gelu = [mm(normed_two, item) for item in up_q]
-    gelu_pairs = [jax.vjp(gelu_exact, item) for item in pre_gelu]
-    activated = [narrow(item[0]) for item in gelu_pairs]
+    below = [0.5 + 0.5 * lax.erf(item * 0.5**0.5) for item in pre_gelu]
+    slopes = [
+        part + item * jnp.exp(-0.5 * item * item) * (0.5 / jnp.pi) ** 0.5
+        for part, item in zip(below, pre_gelu)
+    ]
+    activated = [narrow(item * part) for part, item in zip(below, pre_gelu)]
     after_mlp = after_attn + sum(mm_nt(activated[q], down_q[q]) for q in range(4))
     normed_out = narrow(norm_apply(after_mlp, gain_full[2]))
     logits = [mm(normed_out, item) for item in table_q]
@@ -762,7 +948,7 @@
     mlp_branch = narrow(mlp_grad)
     down_grad = [narrow(mm_tn(mlp_branch, item)) for item in activated]
     up_input = [
-        narrow(gelu_pairs[q][1](mm(mlp_branch, down_q[q]))[0]) for q in range(4)
+        narrow(slopes[q] * mm(mlp_branch, down_q[q])) for q in range(4)
     ]
     up_grad = [narrow(mm_tn(normed_two, item)) for item in up_input]
     normed_two_grad = sum(mm_nt(up_input[q], up_q[q]) for q in range(4))
@@ -801,58 +987,46 @@
         narrow(mm_tn(normed_out, logit_grad[piece]) + mm_tn(embed_scaled, input_hot[piece]))
         for piece in pieces
     ]
-    table_sum, joint_sum, up_sum, down_sum, out_sum = reduce_grads(
-        [table_grad, joint_grad, up_grad, down_grad, out_grad_q], 1
-    )
-    gain_sum = joint_sum[:, head_part : head_part + 3].T
-    reduced = (
-        table_sum.T,
-        joint_sum[:, :head_part],
-        out_sum.T,
-        up_sum,
-        down_sum.T,
-        gain_sum,
-    )
-    local_square = jnp.zeros((), jnp.float32)
-    for grad_item in reduced[:5]:
-        local_square = local_square + jnp.sum(grad_item * grad_item)
-    local_square = local_square + jnp.sum(gain_sum * gain_sum) / parts
-    totals = everyone_sum(jnp.stack([local_square, loss_local, count_local]))
-    square_total, loss_total, count_total = totals[0], totals[1], totals[2]
-    grad_norm = jnp.sqrt(square_total) / count_total
-    clip_scale = jnp.minimum(1.0, clip_at / grad_norm)
-    loss = loss_total / count_total
+    sublane = lax.broadcasted_iota(jnp.int32, (8, 128), 0)
+    facts = jnp.where(sublane == 1, loss_local, jnp.where(sublane == 2, count_local, 0.0))
+    joint_part = joint_grad[0].shape[1]
+    layout = (
+        ((0, 0, vocab_part),),
+        ((2, 0, ff_part), (3, ff_part, ff_part)),
+        ((1, 0, joint_part), (4, joint_part, out_part)),
+    )
+    sums, totals = reduce_grads(
+        layout,
+        [table_grad, joint_grad, up_grad, down_grad, out_grad_q],
+        facts,
+        parts,
+        (2, head_part, joint_part - head_part),
+    )
     step_float = step_count[0].astype(jnp.float32)
-    fix_one = 1.0 - jnp.power(beta_one, step_float)
-    fix_two = 1.0 - jnp.power(beta_two, step_float)
-    masters = (table, joint_weight, output_weight, upward_weight, downward_weight, gains)
-    moments_one = (
-        momentum_table,
-        momentum_joint,
-        momentum_output,
-        momentum_upward,
-        momentum_downward,
-        momentum_gains,
-    )
-    moments_two = (
-        variance_table,
-        variance_joint,
-        variance_output,
-        variance_upward,
-        variance_downward,
-        variance_gains,
-    )
-    updated = []
-    for index in range(6):
-        clipped = reduced[index] / count_total * clip_scale
-        moment_one = beta_one * moments_one[index] + (1.0 - beta_one) * clipped
-        moment_two = beta_two * moments_two[index] + (1.0 - beta_two) * clipped * clipped
-        stepped = moment_one / fix_one / (jnp.sqrt(moment_two / fix_two) + adam_eps)
-        master = masters[index]
-        updated.extend(
-            [moment_one, moment_two, master - rates[index] * (stepped + decays[index] * master)]
-        )
-    return tuple([loss, grad_norm] + updated)
+    fixes = jnp.where(
+        sublane == 0,
+        1.0 / (1.0 - jnp.power(beta_one, step_float)),
+        1.0 / (1.0 - jnp.power(beta_two, step_float)),
+    )
+    plans = (
+        (0, False, 0, rates[0], decays[0]),
+        (2, False, 0, rates[1], decays[1]),
+        (2, True, joint_part, rates[2], decays[2]),
+        (1, False, 0, rates[3], decays[3]),
+        (1, False, ff_part, rates[4], decays[4]),
+        (2, True, head_part, rates[5], decays[5]),
+    )
+    triples = (
+        (table.T, momentum_table.T, variance_table.T),
+        (joint_weight, momentum_joint, variance_joint),
+        (output_weight, momentum_output, variance_output),
+        (upward_weight, momentum_upward, variance_upward),
+        (downward_weight.T, momentum_downward.T, variance_downward.T),
+        (gains, momentum_gains, variance_gains),
+    )
+    updated, results = update_weights(totals, fixes, sums, plans, triples)
+    updated = [item.T if place // 3 in (0, 4) else item for place, item in enumerate(updated)]
+    return tuple([results[0, 0], results[1, 0]] + updated)
 
 
 def solution(mesh):

time: 613 us -> 558 us (0.910)
  other arithmetic: 77.1 us -> 53.9 us
  Pallas kernels: 274 us -> 264 us
  between operations: 14.9 us -> 4.97 us
  matrix products: 168 us -> 176 us
  waiting for transfers between devices: 8.04 us -> 0.47 us
  local copies, waits for them, and re-layouts: 51.3 us -> 44.5 us
  starting transfers between devices: 9.05 us -> 2.71 us
    dot_general x21, matrix products: 45.8 us -> 64.5 us  [mm_tn(): lax.dot_general(left, right, (((0,), (0,)), ((), ())), preferred_element_...]
    dot_general x17, matrix products: 37.9 us -> 22.7 us  [mm(): return jnp.dot(left, right, preferred_element_type=jnp.float32)]
    sub x6 -> x0, other arithmetic: 10.5 us -> none  [per_device(): master - rates[index] * (stepped + decays[index] * master)]
    pallas_call x1 -> x2, Pallas kernels: 154 us -> 144 us  [the longest x1 138 us: reduce_kernel(): pl.pallas_call(functools.partial(reduce_body, layout, parts, gains_at), n...]
    reduce_sum x6 -> x0, other arithmetic: 9.1 us -> none  [the longest x5 7.62 us: per_device(): local_square = local_square + jnp.sum(grad_item * grad_item)]
    ppermute x14 -> x8, waiting for transfers between devices: 8.04 us -> 0.47 us  [swap(): lax.ppermute(value, axis, [(place, place ^ mask) for place in range(size)])]
    slice x5 -> x1, local copies, waits for them, and re-layouts: 7.73 us -> 1.28 us  [per_device(): return tuple([results[0, 0], results[1, 0]] + updated)]
    ppermute x14 -> x8, starting transfers between devices: 9.05 us -> 2.71 us  [swap(): lax.ppermute(value, axis, [(place, place ^ mask) for place in range(size)])]
  transfers between devices with their start and end apart: 14 -> 8, of which waited for: 6 -> 1; matrix products, arithmetic and copies ran while one was open for 13% -> 11% of each run, Pallas kernels for 0% -> 0%
where the time goes in v3:
time: 558 us; the launch traced here: 547 us
  Pallas kernels  264 us (47%)
  matrix products  176 us (32%)
  other arithmetic  53.9 us (10%)
  local copies, waits for them, and re-layouts  44.5 us (8%)
    pallas_call x1, Pallas kernels, reduce_kernel(): pl.pallas_call(functools.partial(reduce_body, layout, parts, gains_at), n...  138 us
    pallas_call x1, Pallas kernels, gather_kernel(): pl.pallas_call(functools.partial(gather_body, items), name='gather_weight...  121 us
    dot_general x21, matrix products, mm_tn(): lax.dot_general(left, right, (((0,), (0,)), ((), ())), preferred_element_...  64.5 us
    dot_general x21, matrix products, mm_nt(): lax.dot_general(left, right, (((1,), (1,)), ((), ())), preferred_element_...  36.3 us
    unnamed x245, local copies, waits for them, and re-layouts  24.1 us
    dot_general x17, matrix products, mm(): return jnp.dot(left, right, preferred_element_type=jnp.float32)  22.7 us
    dot_general x2, matrix products, attend_back(): jnp.einsum('hqk,qhe->khe', probs.astype(jnp.bfloat16), grad_out, preferre...  14.7 us
    convert_element_type x9, other arithmetic, narrow(): return value.astype(jnp.bfloat16)  12.6 us
  transfers between devices with their start and end apart: 8, of which 1 were waited for; matrix products, arithmetic and copies ran while one was open for 11% of the time, Pallas kernels for 0%

profile of v3, /device:TPU:0, one launch (start us, length us, event | category | flops | bytes accessed | tf_op | source)
XLA Modules:
  0.0 547.1 jit_solution(10417015222899985314)
XLA Ops:
  15.2 120.8 %gather_weights.1 = (bf16[768,2048]{1,0:T(8,128)(2,1)}, bf16[768,2048]{1,0:T(8,128)(2,1)}, bf16[768,2048]{1,0:T(8,128)(2,1)}, bf16[768,2048]{1,0:T(8,128)(2,1)},...) custom-call(bf16[96,2048]{1,0:T(8,128)(2,1)} %convert_bitcast_fusion, ...), custom_call_target="tpu_custom_call" | custom-call | tf_op jit(solution)/shard_map/gather_weights/pallas_call | solution.py:255
  139.2 4.0 fusion.17
  161.9 2.6 fusion.119
  166.3 2.8 copy-done
  169.1 2.3 fusion.71
  173.7 2.7 fusion.118
  178.1 2.8 copy-done.1
  181.0 2.5 fusion.72
  185.1 2.3 multiply_reduce_fusion.9
  210.4 5.0 select_reduce_fusion.2
  216.0 7.7 %multiply_convert_fusion.2 = (bf16[512,2048]{1,0:T(8,128)(2,1)}, bf16[512,2048]{1,0:T(8,128)(2,1)S(1)}, bf16[512,2048]{1,0:T(8,128)(2,1)}, bf16[512,2048]{1,0:T(8,128)(2,1)S(1)}) fusion(f32[512,2048]{1,0:T(8,128)S(1)} %get-tuple-element.244, s32[512]{0:T(512)S(1)} %get-tuple-element.205, f32[512]{0:T(512)S(1)} %get-tuple-element.125, ...), kind=kLoop, calls=%fused_computation.30 | loop fusion | flops 25165824 | bytes 25178112 | tf_op jit(solution)/shard_map/convert_element_type | solution.py:703
  223.8 5.4 fusion.128
  273.6 7.2 %fusion.65 = bf16[1024,3,1,64]{0,3,1,2:T(8,128)(2,1)S(1)} fusion(bf16[1024,3,64]{0,2,1:T(8,128)(2,1)S(1)} %bitcast.293, f32[3,1024,1024]{1,2,0:T(8,128)} %copy-done.1, f32[3,1024]{1,0:T(4,128)} %log_add_fusion), kind=kOutput, calls=%fused_computation.148 | convolution fusion | flops 409141248 | bytes 13381632 | tf_op jit(solution)/shard_map/hqk,qhe->khe/dot_general | solution.py:782
  280.8 6.2 %multiply_reduce_fusion = (f32[3,1024]{1,0:T(4,128)S(1)}, f32[3,1024,1024]{1,2,0:T(8,128)S(1)}) fusion(f32[3,1024,1024]{1,2,0:T(8,128)} %copy-done.1, f32[3,1024]{1,0:T(4,128)S(1)} %copy-done.40, bf16[1024,3,64]{0,2,1:T(8,128)(2,1)S(1)} %bitcast.294, bf16[1024,3,3,64]{0,3,2,1:T(8,128)(2,1)} %bitcast.290), kind=kOutput, calls=%fused_computation.1 | convolution fusion | flops 412087296 | bytes 25976832 | tf_op jit(solution)/shard_map/qhe,khe->hqk/dot_general | solution.py:785
  288.0 5.2 multiply_convert_fusion
  293.2 6.0 %fusion.53 = f32[1024,3,64]{0,2,1:T(8,128)} fusion(bf16[3,1024,1024]{1,2,0:T(8,128)(2,1)} %multiply_convert_fusion, bf16[1024,3,3,64]{0,3,2,1:T(8,128)(2,1)} %bitcast.291), kind=kOutput, calls=%fused_computation.137 | convolution fusion | flops 402849792 | bytes 7471104 | tf_op jit(solution)/shard_map/hqk,qhe->khe/dot_general | solution.py:791
  299.1 3.1 fusion.54
  305.4 7.5 %fusion.68 = bf16[1024,3,1,64]{0,3,1,2:T(8,128)(2,1)} fusion(bf16[1024,3,64]{0,2,1:T(8,128)(2,1)S(1)} %bitcast.295, f32[3,1024,1024]{1,2,0:T(8,128)} %copy-done, f32[3,1024]{1,0:T(4,128)S(1)} %log_add_fusion.1), kind=kOutput, calls=%fused_computation.149 | convolution fusion | flops 409141248 | bytes 13381632 | tf_op jit(solution)/shard_map/hqk,qhe->khe/dot_general | solution.py:782
  312.9 6.2 %multiply_reduce_fusion.1 = (f32[3,1024]{1,0:T(4,128)S(1)}, f32[3,1024,1024]{1,2,0:T(8,128)S(1)}) fusion(f32[3,1024,1024]{1,2,0:T(8,128)} %copy-done, f32[3,1024]{1,0:T(4,128)S(1)} %log_add_fusion.1, bf16[1024,3,64]{0,2,1:T(8,128)(2,1)S(1)} %bitcast.296, bf16[1024,3,3,64]{0,3,2,1:T(8,128)(2,1)S(1)} %bitcast.285), kind=kOutput, calls=%fused_computation.4 | convolution fusion | flops 412087296 | bytes 25980928 | tf_op jit(solution)/shard_map/qhe,khe->hqk/dot_general | solution.py:785
  320.0 5.2 multiply_convert_fusion.1
  325.2 5.0 fusion.55
  341.9 2.4 copy.245
  351.3 4.7 fusion.12
  356.0 4.6 fusion.16
  360.6 4.7 fusion.14
  365.3 4.6 fusion.18
  374.9 7.1 %add_convert_fusion.refs_3_ = bf16[768,2048]{1,0:T(8,128)(2,1)} fusion(f32[768,2048]{1,0:T(8,128)} %fusion.12, bf16[512,768]{1,0:T(8,128)(2,1)S(1)} %copy-done.42, bf16[512,2048]{1,0:T(8,128)(2,1)} %get-tuple-element.215), kind=kOutput, calls=%fused_computation.18 | convolution fusion | flops 1613758464 | bytes 12320768 | tf_op jit(solution)/shard_map/dot_general | solution.py:747
  382.0 6.5 %add_convert_fusion.1.refs_2_ = bf16[768,2048]{1,0:T(8,128)(2,1)} fusion(f32[768,2048]{1,0:T(8,128)} %fusion.16, bf16[512,768]{1,0:T(8,128)(2,1)S(1)} %copy-done.42, bf16[512,2048]{1,0:T(8,128)(2,1)S(1)} %copy-done.30), kind=kOutput, calls=%fused_computation.19 | convolution fusion | flops 1613758464 | bytes 12320768 | tf_op jit(solution)/shard_map/dot_general | solution.py:747
  388.5 6.5 %add_convert_fusion.2.refs_1_ = bf16[768,2048]{1,0:T(8,128)(2,1)} fusion(f32[768,2048]{1,0:T(8,128)} %fusion.14, bf16[512,768]{1,0:T(8,128)(2,1)S(1)} %copy-done.42, bf16[512,2048]{1,0:T(8,128)(2,1)S(1)} %copy-done.28), kind=kOutput, calls=%fused_computation.20 | convolution fusion | flops 1613758464 | bytes 12320768 | tf_op jit(solution)/shard_map/dot_general | solution.py:747
  395.0 3.7 add_convert_fusion.3.refs_0_
  400.9 137.9 %reduce_grads.1 = (f32[96,2048]{1,0:T(8,128)}, f32[96,1536]{1,0:T(8,128)}, f32[96,832]{1,0:T(8,128)}, f32[8,128]{1,0:T(8,128)}) custom-call(bf16[768,2048]{1,0:T(8,128)(2,1)} %add_convert_fusion.3.refs_0_, bf16[768,2048]{1,0:T(8,128)(2,1)} %add_convert_fusion.2.refs_1_, bf16[768,2048]{1,0:T(8,128)(2,1)} %add_convert_fusion.1.refs_2_, ...), custom_call_target="tpu_custom_call" | custom-call | tf_op jit(solution)/shard_map/reduce_grads/pallas_call | solution.py:586
  539.6 5.8 %update_weights.1 = (f32[96,2048]{1,0:T(8,128)}, f32[96,2048]{1,0:T(8,128)}, f32[96,2048]{1,0:T(8,128)}, f32[96,576]{1,0:T(8,128)}, f32[96,576]{1,0:T(8,128)}, /...) custom-call(f32[8,128]{1,0:T(8,128)} %get-tuple-element.83.refs_0_, ...), custom_call_target="tpu_custom_call" | custom-call | tf_op jit(solution)/shard_map/update_weights/pallas_call | solution.py:664
  (415 shorter events, 141.1 us)
Async XLA Ops:
  0.7 13.0 %copy-start.21 = (f32[2048,96]{0,1:T(8,128)S(1)}, f32[2048,96]{0,1:T(8,128)}, u32[]{:S(2)}) copy-start(f32[2048,96]{0,1:T(8,128)} %param.28) | copy-start | bytes 2359300
  5.7 132.0 %copy-start.60 = (pred[1024]{0:T(1024)(128)(4,1)}, pred[1024]{0:T(1024)(128)(4,1)S(1)}, u32[]{:S(2)}) copy-start(pred[1024]{0:T(1024)(128)(4,1)S(1)} %broadcast_compare_fusion.1) | copy-start | bytes 3076
  137.6 12.5 %copy-start.51 = (f32[768]{0:T(1024)}, f32[768]{0:T(1024)S(1)}, u32[]{:S(2)}) copy-start(f32[768]{0:T(1024)S(1)} %get-tuple-element.122) | copy-start | bytes 9220
  139.2 6.1 %copy-start.68 = (s32[512]{0:T(512)}, s32[512]{0:T(512)S(1)}, u32[]{:S(2)}) copy-start(s32[512]{0:T(512)S(1)} %get-tuple-element.206) | copy-start | bytes 6148
  139.2 8.1 %copy-start.62 = (s32[512]{0:T(512)}, s32[512]{0:T(512)S(1)}, u32[]{:S(2)}) copy-start(s32[512]{0:T(512)S(1)} %get-tuple-element.209) | copy-start | bytes 6148
  150.3 5.7 %copy-start.4 = (bf16[512,768]{1,0:T(8,128)(2,1)}, bf16[512,768]{1,0:T(8,128)(2,1)S(1)}, u32[]{:S(2)}) copy-start(bf16[512,768]{1,0:T(8,128)(2,1)S(1)} %multiply_convert_fusion.13) | copy-start | bytes 2359300
  154.2 17.5 %collective-permute-start.1 = (bf16[512,576]{0,1:T(8,128)(2,1)S(1)}, bf16[512,576]{0,1:T(8,128)(2,1)S(1)}, u32[]{:S(2)}, u32[]{:S(2)}) collective-permute-start(bf16[512,576]{0,1:T(8,128)(2,1)S(1)} %bitcast.322), channel_id=1, source_target_pairs={{0,1},{1,0},{2,3},{3,2},{4,5},{5,4},{6,7},{7,6},{8,9},{9,8},{10,11... | collective-permute-start | bytes 1769480 | tf_op jit(solution)/shard_map/ppermute | solution.py:64
  158.3 3.4 collective-permute-start
  171.5 13.6 %copy-start.49 = (bf16[512,3,64]{0,2,1:T(8,128)(2,1)}, bf16[512,3,64]{0,2,1:T(8,128)(2,1)S(1)}, u32[]{:S(2)}) copy-start(bf16[512,3,64]{0,2,1:T(8,128)(2,1)S(1)} %get-tuple-element.172) | copy-start | bytes 589828
  171.5 13.1 %collective-permute-start.2 = (bf16[512,192]{0,1:T(8,128)(2,1)S(1)}, bf16[512,192]{0,1:T(8,128)(2,1)}, u32[]{:S(2)}, u32[]{:S(2)}) collective-permute-start(bf16[512,192]{0,1:T(8,128)(2,1)S(1)} %bitcast.332), channel_id=1, source_target_pairs={{0,1},{1,0},{2,3},{3,2},{4,5},{5,4},{6,7},{7,6},{8,9},{9,8},{10,11... | collective-permute-start | bytes 589832 | tf_op jit(solution)/shard_map/ppermute | solution.py:64
  183.5 1.6 collective-permute-start.3
  187.6 6.5 %copy-start.43 = (bf16[512,768]{1,0:T(8,128)(2,1)}, bf16[512,768]{1,0:T(8,128)(2,1)S(1)}, u32[]{:S(2)}) copy-start(bf16[512,768]{1,0:T(8,128)(2,1)S(1)} %multiply_convert_fusion.12) | copy-start | bytes 2359300
  202.1 6.0 %copy-start.41 = (bf16[512,768]{1,0:T(8,128)(2,1)}, bf16[512,768]{1,0:T(8,128)(2,1)S(1)}, u32[]{:S(2)}) copy-start(bf16[512,768]{1,0:T(8,128)(2,1)S(1)} %multiply_convert_fusion.7) | copy-start | bytes 2359300
  223.7 7.3 %copy-start.27 = (bf16[512,2048]{1,0:T(8,128)(2,1)}, bf16[512,2048]{1,0:T(8,128)(2,1)S(1)}, u32[]{:S(2)}) copy-start(bf16[512,2048]{1,0:T(8,128)(2,1)S(1)} %get-tuple-element.216) | copy-start | bytes 6291460
  266.3 5.1 collective-permute-start.5
  266.7 35.6 %collective-permute-start.4 = (bf16[512,192]{1,0:T(8,128)(2,1)}, bf16[512,192]{1,0:T(8,128)(2,1)}, u32[]{:S(2)}, u32[]{:S(2)}) collective-permute-start(bf16[512,192]{1,0:T(8,128)(2,1)} %get-tuple-element.154), channel_id=1, source_target_pairs={{0,1},{1,0},{2,3},{3,2},{4,5},{5,4},{6,7},{7,6},{8,9},{9,8},{10,11... | collective-permute-start | bytes 589832 | tf_op jit(solution)/shard_map/ppermute | solution.py:64
  273.6 7.2 %copy-start.40 = (f32[3,1024]{1,0:T(4,128)S(1)}, f32[3,1024]{1,0:T(4,128)}, u32[]{:S(2)}) copy-start(f32[3,1024]{1,0:T(4,128)} %log_add_fusion) | copy-start | bytes 36868
  273.6 13.4 %slice-start.3 = ((s8[12582912]{0:T(1024)(128)(4,1)}), s8[4194304]{0:T(1024)(128)(4,1)S(1)}, s32[]{:S(2)}) async-start(s8[12582912]{0:T(1024)(128)(4,1)} %bitcast.281), calls=%async_computation.3 | async-start | bytes 8388608
  280.8 6.3 %slice-start.4 = ((s8[12582912]{0:T(1024)(128)(4,1)}), s8[4194304]{0:T(1024)(128)(4,1)S(1)}, s32[]{:S(2)}) async-start(s8[12582912]{0:T(1024)(128)(4,1)} %bitcast.281), calls=%async_computation.4 | async-start | bytes 8388608
  280.8 7.2 %slice-start.5 = ((s8[12582912]{0:T(1024)(128)(4,1)}), s8[4194304]{0:T(1024)(128)(4,1)S(1)}, s32[]{:S(2)}) async-start(s8[12582912]{0:T(1024)(128)(4,1)} %bitcast.281), calls=%async_computation.5 | async-start | bytes 8388608
  293.2 6.0 %copy-start.2 = (bf16[3,1024,1024]{1,2,0:T(8,128)(2,1)S(1)}, bf16[3,1024,1024]{1,2,0:T(8,128)(2,1)}, u32[]{:S(2)}) copy-start(bf16[3,1024,1024]{1,2,0:T(8,128)(2,1)} %multiply_convert_fusion) | copy-start | bytes 18874372
  305.3 13.8 %slice-start = ((s8[12582912]{0:T(1024)(128)(4,1)}), s8[4194304]{0:T(1024)(128)(4,1)S(1)}, s32[]{:S(2)}) async-start(s8[12582912]{0:T(1024)(128)(4,1)} %bitcast.279), calls=%async_computation | async-start | bytes 8388608
  312.9 6.2 %slice-start.1 = ((s8[12582912]{0:T(1024)(128)(4,1)}), s8[4194304]{0:T(1024)(128)(4,1)S(1)}, s32[]{:S(2)}) async-start(s8[12582912]{0:T(1024)(128)(4,1)} %bitcast.279), calls=%async_computation.1 | async-start | bytes 8388608
  312.9 7.1 %slice-start.2 = ((s8[12582912]{0:T(1024)(128)(4,1)}), s8[4194304]{0:T(1024)(128)(4,1)S(1)}, s32[]{:S(2)}) async-start(s8[12582912]{0:T(1024)(128)(4,1)} %bitcast.279), calls=%async_computation.2 | async-start | bytes 8388608
  344.4 3.5 collective-permute-start.6
  344.8 4.2 collective-permute-start.7
  374.9 7.1 %copy-start.30 = (bf16[512,2048]{1,0:T(8,128)(2,1)S(1)}, bf16[512,2048]{1,0:T(8,128)(2,1)}, u32[]{:S(2)}) copy-start(bf16[512,2048]{1,0:T(8,128)(2,1)} %get-tuple-element.217) | copy-start | bytes 6291460
  382.0 6.5 %copy-start.28 = (bf16[512,2048]{1,0:T(8,128)(2,1)S(1)}, bf16[512,2048]{1,0:T(8,128)(2,1)}, u32[]{:S(2)}) copy-start(bf16[512,2048]{1,0:T(8,128)(2,1)} %copy-done.27) | copy-start | bytes 6291460
  382.0 13.0 %slice-start.6 = ((s8[6291456]{0:T(1024)(128)(4,1)}), s8[4194304]{0:T(1024)(128)(4,1)S(1)}, s32[]{:S(2)}) async-start(s8[6291456]{0:T(1024)(128)(4,1)} %bitcast.343), calls=%async_computation.6 | async-start | bytes 8388608
  388.5 6.5 %copy-start.26 = (bf16[512,2048]{1,0:T(8,128)(2,1)S(1)}, bf16[512,2048]{1,0:T(8,128)(2,1)}, u32[]{:S(2)}) copy-start(bf16[512,2048]{1,0:T(8,128)(2,1)} %copy-done.25) | copy-start | bytes 6291460
  388.5 6.5 %slice-start.7 = ((s8[6291456]{0:T(1024)(128)(4,1)}), s8[2097152]{0:T(1024)(128)(4,1)S(1)}, s32[]{:S(2)}) async-start(s8[6291456]{0:T(1024)(128)(4,1)} %bitcast.343), calls=%async_computation.7 | async-start | bytes 4194304
  400.9 137.9 %copy-start.70 = (f32[8]{0:T(128)S(1)}, f32[8]{0:T(128)}, u32[]{:S(2)}) copy-start(f32[8]{0:T(128)} %compare_select_fusion) | copy-start | bytes 100
  (95 other events, 224.1 us)
